TPU v7x, 128 devices: a whole 4x4x4 slice. The times are simulated.
128 devices in a mesh: dp: 8 (over z, core), seq: 8 (over x, y_lo), mp: 2 (over y_hi).
Axes of the slice: x: 4, y: 4 (y_hi: 2, y_lo: 2; y = y_hi * 2 + y_lo), z: 4, core: 2. Of those that a mesh axis runs over, the one named last changes fastest.
Arguments:
- residual: bfloat16 [24576, 3072], P(('dp', 'seq'), 'mp'), parts along dimension 0, may hold values from -10 to 10
- queries: bfloat16 [24576, 3072], P(('dp', 'seq', 'mp')), parts along dimension 0, may hold values from -6 to 6
- keys: bfloat16 [24576, 3072], P(('dp', 'seq', 'mp')), parts along dimension 0, may hold values from -6 to 6
- values: bfloat16 [24576, 3072], P(('dp', 'seq', 'mp')), parts along dimension 0, may hold values from -6 to 6
- video_ids: int32 [24576], P(('dp', 'seq', 'mp')), parts along dimension 0, may hold values from 0 to 3, never falling along the last dimension, each value on 1 to 1536 neighbouring positions
- timestep: int32 [8], P('dp'), parts along dimension 0, may hold values from 0 to 49
- modulation: float32 [50, 3, 3072], P(None, None, 'mp'), may hold values from -4 to 4
- out_weight: bfloat16 [3072, 3072], P(None, 'mp'), may hold values from -0.109375 to 0.109375
Outputs:
- hidden_out: bfloat16 [24576, 3072], P(('dp', 'seq'), 'mp'), parts along dimension 0
- mlp_input: bfloat16 [24576, 3072], P(('dp', 'seq'), 'mp'), parts along dimension 0
There are 8 independent parts, one for each index of `dp`. A program takes and returns all parts, laid end to end along the dimension named above; an argument that names none is the same for every part. Nothing has to cross between parts.
Inputs may be any that keep to these rules, and one draw needn't show every extreme that they name: `video_ids`: video ids never fall along the tokens; each video holds 1 to 1536 tokens and one holds exactly 1536.
All inputs are finite; a program needn't handle non-finite values.
Results may differ from a plain program's by a relative error of at most 0.005.
Values may be sent and summed in bfloat16 or wider, within the bound.
No kernel may reach another device: no remote copies, remote signals or barrier semaphores. Data moves between devices by JAX's collectives and lax.ppermute only.
A program may use at most 256 MiB of HBM per device.

v0:
```python
import jax
import jax.numpy as jnp
from jax import lax
from jax.sharding import PartitionSpec as P

HEAD_DIM = 128


def attend(carry, q_rows, q_ids, key_rows, value_rows, key_ids):
    top, total, summed = carry
    rows = q_rows.shape[0]
    count = key_rows.shape[0]
    heads = q_rows.shape[1] // HEAD_DIM
    factor = 1.0 / HEAD_DIM**0.5
    q_heads = q_rows.reshape(rows, heads, HEAD_DIM)
    k_heads = key_rows.reshape(count, heads, HEAD_DIM)
    v_heads = value_rows.reshape(count, heads, HEAD_DIM)
    same = (q_ids[:, None] == key_ids[None, :])[None]
    new_top, new_total, new_summed = ([], [], [])
    for first in range(0, heads, 3):
        score = (
            jnp.einsum(
                "thd,nhd->htn",
                q_heads[:, first : first + 3],
                k_heads[:, first : first + 3],
                preferred_element_type=jnp.float32,
            )
            * factor
        )
        score = jnp.where(same, score, -1e30)
        old_top = top[first : first + 3]
        peak = jnp.maximum(old_top, jnp.max(score, axis=2))
        weight = jnp.where(same, jnp.exp(score - peak[:, :, None]), 0.0)
        new_top.append(peak)
        new_total.append(jnp.sum(weight, axis=2))
        part_sum = jnp.einsum(
            "htn,nhd->htd",
            weight.astype(jnp.bfloat16),
            v_heads[:, first : first + 3],
            preferred_element_type=jnp.float32,
        )
        new_summed.append(part_sum)
    return (
        jnp.concatenate(new_top, 0),
        jnp.concatenate(new_total, 0),
        jnp.concatenate(new_summed, 0),
    )


def attend_maybe(carry, q_rows, q_ids, key_rows, value_rows, key_ids):
    return attend(carry, q_rows, q_ids, key_rows, value_rows, key_ids)


def start_state(q_rows):
    rows = q_rows.shape[0]
    heads = q_rows.shape[1] // HEAD_DIM
    return (
        jnp.full((heads, rows), -1e30, jnp.float32),
        jnp.zeros((heads, rows), jnp.float32),
        jnp.zeros((heads, rows, HEAD_DIM), jnp.float32),
    )


def finish(state, q_rows):
    top, total, summed = state
    rows = q_rows.shape[0]
    heads = q_rows.shape[1] // HEAD_DIM
    result = summed / total[:, :, None]
    return result.transpose(1, 0, 2).reshape(rows, heads * HEAD_DIM).astype(jnp.bfloat16)


def local(residual, queries, keys, values, video_ids, timestep, modulation, out_weight):
    steps_count = modulation.shape[0]
    picker = (jnp.arange(steps_count, dtype=jnp.int32) == timestep[0]).astype(jnp.float32)
    mod_rows = jnp.einsum("s,scd->cd", picker, modulation, precision=lax.Precision.HIGHEST)
    gate = mod_rows[0]
    shift = mod_rows[1]
    scale = mod_rows[2]
    width = queries.shape[1]
    state = attend_maybe(
        start_state(queries),
        queries,
        video_ids,
        lax.all_gather(keys, ("seq", "mp"), axis=0, tiled=True),
        lax.all_gather(values, ("seq", "mp"), axis=0, tiled=True),
        lax.all_gather(video_ids, ("seq", "mp"), axis=0, tiled=True),
    )
    attended = finish(state, queries)
    projected = jnp.dot(
        lax.all_gather(attended, "mp", axis=0, tiled=True),
        out_weight,
        preferred_element_type=jnp.float32,
    )
    stream = residual.astype(jnp.float32) + gate[None, :] * projected
    row_sum = jnp.sum(stream, axis=1, keepdims=True)
    row_sq = jnp.sum(stream * stream, axis=1, keepdims=True)
    row_sum, row_sq = lax.psum((row_sum, row_sq), "mp")
    mean = row_sum / width
    var = row_sq / width - mean * mean
    normed = (stream - mean) * lax.rsqrt(var + 1e-06) * (1.0 + scale[None, :]) + shift[None, :]
    return (stream.astype(jnp.bfloat16), normed.astype(jnp.bfloat16))


def solution(mesh):
    return jax.shard_map(
        local,
        mesh=mesh,
        in_specs=(
            P(("dp", "seq"), "mp"),
            P(("dp", "seq", "mp"), None),
            P(("dp", "seq", "mp"), None),
            P(("dp", "seq", "mp"), None),
            P(("dp", "seq", "mp")),
            P("dp"),
            P(None, None, "mp"),
            P(None, "mp"),
        ),
        out_specs=(P(("dp", "seq"), "mp"), P(("dp", "seq"), "mp")),
        check_vma=False,
    )
```

profile of v0, /device:TPU:38, one launch (start us, length us, event | category | flops | bytes accessed | tf_op | source)
XLA Modules:
  0.0 988.0 jit_solution(17586032627797052202)
XLA Ops:
  13.0 98.5 %all-reduce = s32[3072]{0:T(1024)S(1)} all-reduce(s32[3072]{0:T(1024)S(1)} %dynamic-update-slice), channel_id=1, replica_groups=mesh['dp'=8,'seq'=8,'mp'=2] {'seq','mp'}, use_global_device_ids=true, to_apply=%add | all-reduce | flops 3072 | bytes 24576
  113.3 292.7 %all-gather.4.cloned.1.call-done = bf16[3072,3072]{1,0:T(8,128)(2,1)} async-done(((bf16[192,3072]{1,0:T(8,128)(2,1)}), bf16[3072,3072]{1,0:T(8,128)(2,1)}) %all-gather.4.cloned.1.call-update) | async-done | bytes 18874384 | tf_op jit(solution)/shard_map/all_gather | solution.py:84
  406.1 24.6 %copy.38 = bf16[3072,3072]{0,1:T(8,128)(2,1)} copy(bf16[3072,3072]{1,0:T(8,128)(2,1)} %all-gather.4.cloned.1.call-done) | data formatting | bytes 37748736 | tf_op jit(solution)/shard_map/all_gather | solution.py:84
  433.6 10.7 %fusion.7 = (f32[3,192]{1,0:T(4,128)S(1)}, f32[3,192]{1,0:T(4,128)S(1)}, f32[3,192,3072]{2,1,0:T(8,128)}) fusion(pred[192,3072]{1,0:T(8,128)(4,1)S(1)} %broadcast_compare_fusion, f32[3,192,3072]{2,1,0:T(8,128)S(1)} %fusion.71, bf16[3072,24,128]{0,2,1:T(8,128)(2,1)} %bitcast.23, bf16[192,3,128]{2,1,0:T(4,128)(2,1)S(1)} %copy-done.4), kind=kOutput, calls=%fused_computation.23 | convolution fusion | flops 463600512 | bytes 17256960 | tf_op jit(solution)/shard_map/thd,nhd->htn/dot_general | solution.py:22
  444.3 3.9 fusion.65
  448.2 3.9 fusion.62
  452.2 4.1 fusion.59
  456.3 3.9 fusion.56
  460.2 3.9 fusion.53
  464.1 336.0 %all-gather.6.cloned.1.call-done = bf16[3072,3072]{1,0:T(8,128)(2,1)} async-done(((bf16[192,3072]{1,0:T(8,128)(2,1)}), bf16[3072,3072]{1,0:T(8,128)(2,1)}) %all-gather.6.cloned.1.call-update) | async-done | bytes 18874384 | tf_op jit(solution)/shard_map/all_gather | solution.py:85
  800.1 35.7 %copy.40 = bf16[3072,3072]{0,1:T(8,128)(2,1)} copy(bf16[3072,3072]{1,0:T(8,128)(2,1)} %all-gather.6.cloned.1.call-done) | data formatting | bytes 37748736 | tf_op jit(solution)/shard_map/all_gather | solution.py:85
  835.9 6.6 fusion.73
  842.5 20.3 %fusion.22 = (f32[3,192]{1,0:T(4,128)S(1)}, f32[3,192]{1,0:T(4,128)S(1)}, f32[3,192]{1,0:T(4,128)S(1)}, f32[3,192]{1,0:T(4,128)S(1)}, f32[3,192]{1,0:T(4,128)S(1...) fusion(f32[3,192,3072]{2,1,0:T(8,128)} %get-tuple-element.37, ...), kind=kOutput, calls=%fused_computation.38 | convolution fusion | flops 502525440 | bytes 59742720 | tf_op jit(solution)/shard_map/thd,nhd->htn/dot_general | solution.py:22
  862.8 6.6 fusion.78
  869.4 6.6 fusion.83
  876.0 4.4 fusion.88
  880.4 6.6 fusion.93
  887.0 6.6 fusion.98
  893.6 16.4 %fusion.20 = (f32[3,192]{1,0:T(4,128)S(1)}, f32[3,192]{1,0:T(4,128)S(1)}, f32[3,192]{1,0:T(4,128)S(1)}, f32[3,192]{1,0:T(4,128)S(1)}, f32[3,192]{1,0:T(4,128)S(1)}, /*index=5*/f32[3,192]{1,0:T(4,128)S(1)}) fusion(f32[3,192,3072]{2,1,0:T(8,128)S(1)} %copy-done.3, f32[3,192]{1,0:T(4,128)S(1)} %broadcast_maximum_fusion.1, ...), kind=kLoop, calls=%fused_computation.36 | loop fusion | flops 53080704 | bytes 43084800 | tf_op jit(solution)/shard_map/reduce_sum | solution.py:35
  910.0 4.5 fusion.103
  914.4 6.4 fusion.108
  925.5 38.3 %all-gather.8.cloned.1.call-done = bf16[384,3072]{1,0:T(8,128)(2,1)} async-done(((bf16[192,3072]{1,0:T(8,128)(2,1)}), bf16[384,3072]{1,0:T(8,128)(2,1)}) %all-gather.8.cloned.1.call-update) | async-done | bytes 2359312 | tf_op jit(solution)/shard_map/all_gather | solution.py:90
  963.8 8.8 fusion.152
  972.5 6.4 all-reduce.1
  (53 shorter events, 15.9 us)
Async XLA Ops:
  7.2 917.8 %copy-start = (f32[50,3,1536]{2,0,1:T(8,128)S(1)}, f32[50,3,1536]{2,0,1:T(8,128)}, u32[]{:S(2)}) copy-start(f32[50,3,1536]{2,0,1:T(8,128)} %param.14) | copy-start | bytes 2764804
  7.2 105.8 %copy-start.6 = (s32[192]{0:T(256)S(1)}, s32[192]{0:T(256)}, u32[]{:S(2)}) copy-start(s32[192]{0:T(256)} %param.12) | copy-start | bytes 2308
  7.2 398.9 %all-gather.4.cloned.1.call-start = ((), (), s32[]{:S(2)}) async-start(), calls=%async_computation | async-start | bytes 20054016 | tf_op jit(solution)/shard_map/all_gather | solution.py:84
  7.9 792.2 %all-gather.6.cloned.1.call-start = ((), (), s32[]{:S(2)}) async-start(), calls=%async_computation.1 | async-start | bytes 20054016 | tf_op jit(solution)/shard_map/all_gather | solution.py:85
  8.7 955.1 %all-gather.8.cloned.1.call-start = ((), (), s32[]{:S(2)}) async-start(), calls=%async_computation.2 | async-start | bytes 3538944 | tf_op jit(solution)/shard_map/all_gather | solution.py:90
  430.7 2.9 copy-start.4
  430.7 13.6 %copy-start.1 = (bf16[3072,3072]{0,1:T(8,128)(2,1)S(1)}, bf16[3072,3072]{0,1:T(8,128)(2,1)}, u32[]{:S(2)}) copy-start(bf16[3072,3072]{0,1:T(8,128)(2,1)} %copy.38) | copy-start | bytes 56623108
  433.6 10.7 %copy-start.2 = (f32[3,192,3072]{2,1,0:T(8,128)}, f32[3,192,3072]{2,1,0:T(8,128)S(1)}, u32[]{:S(2)}) copy-start(f32[3,192,3072]{2,1,0:T(8,128)S(1)} %fusion.71) | copy-start | bytes 21233668
  835.9 6.6 copy-start.3
  835.9 6.6 copy-start.5
  862.8 13.2 %slice-start.2 = ((s8[7077888]{0:T(1024)(128)(4,1)}), s8[4194304]{0:T(1024)(128)(4,1)S(1)}, s32[]{:S(2)}) async-start(s8[7077888]{0:T(1024)(128)(4,1)} %bitcast.32), calls=%async_computation.5 | async-start | bytes 8388608
  869.4 6.6 slice-start.3
  880.4 13.1 %slice-start = ((s8[7077888]{0:T(1024)(128)(4,1)}), s8[4194304]{0:T(1024)(128)(4,1)S(1)}, s32[]{:S(2)}) async-start(s8[7077888]{0:T(1024)(128)(4,1)} %bitcast.30), calls=%async_computation.3 | async-start | bytes 8388608
  887.0 6.6 slice-start.1
Sparse Core Ops, SparseCore 0:
  9.6 396.4 all-gather.3
  407.7 392.3 all-gather.5
  924.4 39.3 all-gather.7
where the time goes:
time: 998 us; the launch traced here: 988 us
  waiting for transfers between devices  668 us (67%)
  matrix products  111 us (11%)
  blocking collectives  105 us (11%)
  local copies, waits for them, and re-layouts  65.7 us (7%)
  other arithmetic  22 us (2%)
  between operations  15.7 us (2%)
    all_gather x1, waiting for transfers between devices, local(): lax.all_gather(values, ('seq', 'mp'), axis=0, tiled=True)  336 us
    all_gather x1, waiting for transfers between devices, local(): lax.all_gather(keys, ('seq', 'mp'), axis=0, tiled=True)  293 us
    unnamed x1, blocking collectives  98.5 us
    dot_general x8, matrix products, attend(): jnp.einsum('thd,nhd->htn', q_heads[:, first:first + 3], k_heads[:, first:...  53.6 us
    dot_general x8, matrix products, attend(): jnp.einsum('htn,nhd->htd', weight.astype(jnp.bfloat16), v_heads[:, first:...  48.2 us
    all_gather x1, waiting for transfers between devices, local(): lax.all_gather(attended, 'mp', axis=0, tiled=True)  38.3 us
    all_gather x1, local copies, waits for them, and re-layouts, local(): lax.all_gather(values, ('seq', 'mp'), axis=0, tiled=True)  35.7 us
    all_gather x1, local copies, waits for them, and re-layouts, local(): lax.all_gather(keys, ('seq', 'mp'), axis=0, tiled=True)  24.6 us
  transfers between devices with their start and end apart: 3, of which 3 were waited for; matrix products, arithmetic and copies ran while one was open for 6% of the time, Pallas kernels for 0%

commit v1 on v0

v1 whole, which is shorter than its diff:
```python
import functools
import math

import jax
import jax.numpy as jnp
from jax import lax
from jax.experimental import pallas as pl
from jax.experimental.pallas import tpu as pltpu
from jax.sharding import PartitionSpec as P

HEAD_DIM = 128
SHARDS = 16
ROWS = 192
HALF = ROWS // 2
TOKENS = SHARDS * ROWS
QF, KF, KM, VF, VM, QM, ID = 0, 192, 384, 576, 768, 960, 1056
SENT = 1072
BACK = 3 * ROWS
TILE = 512
BIG = 32768.0
SCALE = math.log2(math.e) / math.sqrt(HEAD_DIM)
F32 = jnp.float32
BF16 = jnp.bfloat16


def pack_kernel(q_ref, k_ref, v_ref, id_ref, out_ref):
    for m in range(2):
        full = slice(2 * m * HEAD_DIM, (2 * m + 1) * HEAD_DIM)
        mid = slice(HEAD_DIM, 2 * HEAD_DIM)
        out_ref[m, QF:KF] = q_ref[:, full]
        out_ref[m, KF:KM] = k_ref[:, full]
        out_ref[m, KM:VF] = k_ref[:, mid]
        out_ref[m, VF:VM] = v_ref[:, full]
        out_ref[m, VM:QM] = v_ref[:, mid]
        out_ref[m, QM:ID] = q_ref[m * HALF : (m + 1) * HALF, mid]
        out_ref[m, ID:SENT] = id_ref[...]


def pack(queries, keys, values, id_rows):
    heads3 = pl.BlockSpec((ROWS, 3 * HEAD_DIM), lambda s: (0, s))
    return pl.pallas_call(
        pack_kernel,
        grid=(SHARDS // 2,),
        in_specs=[heads3, heads3, heads3, pl.BlockSpec((SENT - ID, HEAD_DIM), lambda s: (0, 0))],
        out_specs=pl.BlockSpec((2, SENT, HEAD_DIM), lambda s: (s, 0, 0)),
        out_shape=jax.ShapeDtypeStruct((SHARDS, SENT, HEAD_DIM), BF16),
        name="pack",
    )(queries, keys, values, id_rows)


def attend_kernel(mp_ref, got, out_ref, kf, km, vf, vm, qf, qm, ids, bounds, sem):
    t = pl.program_id(0)
    left = pl.ds(0, HEAD_DIM)
    right = pl.ds(HEAD_DIM, HEAD_DIM)

    @pl.when(t == 0)
    def _():
        copies = []
        for b in range(SHARDS):
            rows = pl.ds(b * ROWS, ROWS)
            half = pl.ds(b * HALF, HALF)
            for n, (first, count, ref, dst) in enumerate(
                (
                    (ID, SENT - ID, ids, None),
                    (QF, ROWS, qf, rows),
                    (QM, HALF, qm, half),
                    (KF, ROWS, kf, rows),
                    (KM, ROWS, km, rows),
                    (VF, ROWS, vf, rows),
                    (VM, ROWS, vm, rows),
                )
            ):
                to = ref.at[b] if dst is None else ref.at[dst, left]
                copy = pltpu.make_async_copy(got.at[b, pl.ds(first, count)], to, sem.at[n, b])
                copy.start()
                copies.append((n, copy))
        tail = pl.ds(TOKENS, TILE)
        for ref in (kf, km, vf, vm):
            ref[tail, left] = jnp.zeros((TILE, HEAD_DIM), BF16)
        for ref in (vf, vm):
            ref[:, right] = jnp.ones((TOKENS + TILE, HEAD_DIM), BF16)
        for n, copy in copies:
            if n == 0:
                copy.wait()
        every = ids[...].astype(F32)
        for v in range(3):
            bounds[v] = jnp.sum((every <= v + 0.5).astype(F32)).astype(jnp.int32)
        lane = lax.broadcasted_iota(jnp.int32, (1, HEAD_DIM), 1)
        c0, c1, c2 = bounds[0], bounds[1], bounds[2]
        low = jnp.where(lane == 0, 0, jnp.where(lane == 1, c0, jnp.where(lane == 2, c1, c2)))
        high = jnp.where(lane == 0, c0, jnp.where(lane == 1, c1, jnp.where(lane == 2, c2, TOKENS)))
        none = lane > 3

        def fill(i, _):
            rows = pl.ds(pl.multiple_of(i * ROWS, ROWS), ROWS)
            token = lax.broadcasted_iota(jnp.int32, (ROWS, HEAD_DIM), 0) + i * ROWS
            inside = (token >= low) & (token < high)
            key = jnp.where(inside | none, 0.0, -BIG).astype(BF16)
            kf[rows, right] = key
            km[rows, right] = key
            qf[rows, right] = jnp.where(inside & ~none, 1.0, 0.0).astype(BF16)
            half = pl.ds(pl.multiple_of(i * HALF, HALF), HALF)
            mine = pl.ds(pl.multiple_of(i * ROWS + mp_ref[0] * HALF, HALF), HALF)
            qm[half, right] = qf[mine, right]
            return 0

        lax.fori_loop(0, SHARDS, fill, 0)
        outside = jnp.where(lane > 3, 0.0, -BIG).astype(BF16)
        for ref in (kf, km):
            ref[tail, right] = jnp.broadcast_to(outside, (TILE, HEAD_DIM))
        for n, copy in copies:
            if n:
                copy.wait()

    c0, c1, c2 = bounds[0], bounds[1], bounds[2]
    first = t * (2 * ROWS)
    last = first + (2 * ROWS - 1)
    low = jnp.where(first >= c2, c2, jnp.where(first >= c1, c1, jnp.where(first >= c0, c0, 0)))
    high = jnp.where(last < c0, c0, jnp.where(last < c1, c1, jnp.where(last < c2, c2, TOKENS)))
    low = (low // 16) * 16
    steps = (high - low + TILE - 1) // TILE

    q_full = qf[pl.ds(pl.multiple_of(first, 2 * ROWS), 2 * ROWS), :]
    q_mid = qm[pl.ds(pl.multiple_of(t * ROWS, ROWS), ROWS), :]

    def one(q, k, v, top, acc):
        score = lax.dot_general(q, k, (((1,), (1,)), ((), ())), preferred_element_type=F32)
        peak = jnp.maximum(top, jnp.max(score, axis=1, keepdims=True))
        weight = jnp.exp2((score - peak) * SCALE).astype(BF16)
        kept = jnp.exp2((top - peak) * SCALE)
        return peak, acc * kept + jnp.dot(weight, v, preferred_element_type=F32)

    def step(i, carry):
        top_full, acc_full, top_mid, acc_mid = carry
        at = pl.ds(pl.multiple_of(low + i * TILE, 16), TILE)
        return one(q_full, kf[at, :], vf[at, :], top_full, acc_full) + one(q_mid, km[at, :], vm[at, :], top_mid, acc_mid)

    start = []
    for rows in (2 * ROWS, ROWS):
        start += [jnp.full((rows, 1), -1e30, F32), jnp.zeros((rows, 2 * HEAD_DIM), F32)]
    _, acc_full, _, acc_mid = lax.fori_loop(0, steps, step, tuple(start))
    for acc, at in ((acc_full, slice(0, 2 * ROWS)), (acc_mid, slice(2 * ROWS, BACK))):
        result = (acc[:, :HEAD_DIM] / acc[:, HEAD_DIM:]).astype(BF16)
        out_ref[0, at] = result
        out_ref[1, at] = result


def attend(mp_index, got):
    long = pltpu.VMEM((TOKENS + TILE, 2 * HEAD_DIM), BF16)
    return pl.pallas_call(
        attend_kernel,
        grid=(SHARDS // 2,),
        in_specs=[pl.BlockSpec(memory_space=pltpu.SMEM), pl.BlockSpec(memory_space=pl.ANY)],
        out_specs=pl.BlockSpec((2, BACK, HEAD_DIM), lambda t: (t, 0, 0)),
        out_shape=jax.ShapeDtypeStruct((SHARDS, BACK, HEAD_DIM), BF16),
        scratch_shapes=[
            long,
            long,
            long,
            long,
            pltpu.VMEM((TOKENS, 2 * HEAD_DIM), BF16),
            pltpu.VMEM((TOKENS // 2, 2 * HEAD_DIM), BF16),
            pltpu.VMEM((SHARDS, SENT - ID, HEAD_DIM), BF16),
            pltpu.SMEM((4,), jnp.int32),
            pltpu.SemaphoreType.DMA((7, SHARDS)),
        ],
        name="attend",
    )(mp_index, got)


def project_kernel(got, w_ref, res_ref, mod_ref, hidden_ref, stream_ref, stat_ref, attended, sums):
    j = pl.program_id(0)

    @pl.when(j == 0)
    def _():
        for s in range(SHARDS // 2):
            mid = slice((3 * s + 1) * HEAD_DIM, (3 * s + 2) * HEAD_DIM)
            for m in range(2):
                full = slice((3 * s + 2 * m) * HEAD_DIM, (3 * s + 2 * m + 1) * HEAD_DIM)
                d = 2 * s + m
                attended[:, full] = got[d, : 2 * ROWS]
                for b in range(2):
                    attended[b * ROWS + m * HALF : b * ROWS + (m + 1) * HALF, mid] = got[
                        d, 2 * ROWS + b * HALF : 2 * ROWS + (b + 1) * HALF
                    ]
        sums[...] = jnp.zeros_like(sums)

    projected = jnp.dot(attended[...], w_ref[...], preferred_element_type=F32)
    stream = res_ref[...].astype(F32) + mod_ref[0:1, :] * projected
    hidden_ref[...] = stream.astype(BF16)
    stream_ref[...] = stream
    one, two = sums[0], sums[1]
    for c in range(stream.shape[1] // HEAD_DIM):
        part = stream[:, c * HEAD_DIM : (c + 1) * HEAD_DIM]
        one = one + part
        two = two + part * part
    sums[0] = one
    sums[1] = two

    @pl.when(j == pl.num_programs(0) - 1)
    def _():
        stat_ref[...] = jnp.zeros_like(stat_ref)
        stat_ref[0:1, :] = jnp.sum(sums[0].T, axis=0, keepdims=True)
        stat_ref[1:2, :] = jnp.sum(sums[1].T, axis=0, keepdims=True)


def project(got, out_weight, residual, mod_rows):
    width, cols = out_weight.shape
    rows = residual.shape[0]
    block = 512
    column = lambda j: (0, j)
    return pl.pallas_call(
        project_kernel,
        grid=(cols // block,),
        in_specs=[
            pl.BlockSpec((SHARDS, BACK, HEAD_DIM), lambda j: (0, 0, 0)),
            pl.BlockSpec((width, block), column),
            pl.BlockSpec((rows, block), column),
            pl.BlockSpec((3, block), column),
        ],
        out_specs=[
            pl.BlockSpec((rows, block), column),
            pl.BlockSpec((rows, block), column),
            pl.BlockSpec((8, rows), lambda j: (0, 0)),
        ],
        out_shape=[
            jax.ShapeDtypeStruct((rows, cols), BF16),
            jax.ShapeDtypeStruct((rows, cols), F32),
            jax.ShapeDtypeStruct((8, rows), F32),
        ],
        scratch_shapes=[pltpu.VMEM((rows, width), BF16), pltpu.VMEM((2, rows, HEAD_DIM), F32)],
        name="project",
    )(got, out_weight, residual, mod_rows)


def norm_kernel(width, stream_ref, mine_ref, other_ref, mod_ref, out_ref):
    stats = mine_ref[...] + other_ref[...]
    mean = stats[0:1, :] / width
    var = stats[1:2, :] / width - mean * mean
    rows = mean.shape[1]
    mean = jnp.broadcast_to(mean, (HEAD_DIM, rows)).T
    inv = jnp.broadcast_to(lax.rsqrt(var + 1e-06), (HEAD_DIM, rows)).T
    for c in range(stream_ref.shape[1] // HEAD_DIM):
        at = slice(c * HEAD_DIM, (c + 1) * HEAD_DIM)
        shift = mod_ref[1:2, at]
        scale = mod_ref[2:3, at]
        out_ref[:, at] = ((stream_ref[:, at] - mean) * inv * (1.0 + scale) + shift).astype(BF16)


def norm(stream, mine, other, mod_rows, width):
    rows, cols = stream.shape
    block = 768
    column = lambda j: (0, j)
    whole = pl.BlockSpec((8, rows), lambda j: (0, 0))
    return pl.pallas_call(
        functools.partial(norm_kernel, width),
        grid=(cols // block,),
        in_specs=[pl.BlockSpec((rows, block), column), whole, whole, pl.BlockSpec((3, block), column)],
        out_specs=pl.BlockSpec((rows, block), column),
        out_shape=jax.ShapeDtypeStruct((rows, cols), BF16),
        name="norm",
    )(stream, mine, other, mod_rows)


def local(residual, queries, keys, values, video_ids, timestep, modulation, out_weight):
    axes = ("seq", "mp")
    mod_rows = lax.dynamic_index_in_dim(modulation, timestep[0], 0, keepdims=False)
    spare = jnp.full(((SENT - ID) * HEAD_DIM - ROWS,), 7, jnp.int32)
    id_rows = jnp.concatenate([video_ids, spare]).reshape(SENT - ID, HEAD_DIM).astype(BF16)
    got = lax.all_to_all(pack(queries, keys, values, id_rows), axes, 0, 0)
    mp_index = lax.axis_index("mp").astype(jnp.int32).reshape(1)
    back = lax.all_to_all(attend(mp_index, got), axes, 0, 0)
    hidden, stream, mine = project(back, out_weight, residual, mod_rows)
    other = lax.ppermute(mine, "mp", [(0, 1), (1, 0)])
    return hidden, norm(stream, mine, other, mod_rows, queries.shape[1])


def solution(mesh):
    return jax.shard_map(
        local,
        mesh=mesh,
        in_specs=(
            P(("dp", "seq"), "mp"),
            P(("dp", "seq", "mp"), None),
            P(("dp", "seq", "mp"), None),
            P(("dp", "seq", "mp"), None),
            P(("dp", "seq", "mp")),
            P("dp"),
            P(None, None, "mp"),
            P(None, "mp"),
        ),
        out_specs=(P(("dp", "seq"), "mp"), P(("dp", "seq"), "mp")),
        check_vma=False,
    )
```

time: 998 us -> 196 us (0.20)
  the two profiles are of different devices: /device:TPU:38 before, /device:TPU:41 now
where the time goes in v1:
time: 196 us; the launch traced here: 193 us
  waiting for transfers between devices  115 us (59%)
  Pallas kernels  56.6 us (29%)
  starting transfers between devices  16.5 us (8%)
  local copies, waits for them, and re-layouts  3.26 us (2%)
    all_to_all x1, waiting for transfers between devices, local(): got = lax.all_to_all(pack(queries, keys, values, id_rows), axes, 0, 0)  79.6 us
    pallas_call x1, Pallas kernels, attend(): pl.pallas_call(attend_kernel, grid=(SHARDS // 2,), in_specs=[pl.BlockSpec...  36.6 us
    all_to_all x1, waiting for transfers between devices, local(): back = lax.all_to_all(attend(mp_index, got), axes, 0, 0)  31.4 us
    pallas_call x1, Pallas kernels, project(): pl.pallas_call(project_kernel, grid=(cols // block,), in_specs=[pl.BlockS...  10.2 us
    all_to_all x1, starting transfers between devices, local(): back = lax.all_to_all(attend(mp_index, got), axes, 0, 0)  9.2 us
    pallas_call x1, Pallas kernels, pack(): pl.pallas_call(pack_kernel, grid=(SHARDS // 2,), in_specs=[heads3, heads3...  6.9 us
    all_to_all x1, starting transfers between devices, local(): got = lax.all_to_all(pack(queries, keys, values, id_rows), axes, 0, 0)  6.83 us
  transfers between devices with their start and end apart: 3, of which 3 were waited for; matrix products, arithmetic and copies ran while one was open for 0% of the time, Pallas kernels for 0%

profile of v1, /device:TPU:41, one launch (start us, length us, event | category | flops | bytes accessed | tf_op | source)
XLA Modules:
  0.0 193.2 jit_solution(5404913770311798152)
XLA Ops:
  0.6 0.0 copy-start
  0.6 0.8 convert.4
  1.4 0.6 pad_bitcast_fusion.id_ref
  2.0 6.9 %pack.1 = bf16[16,1072,128]{2,1,0:T(8,128)(2,1)} custom-call(bf16[192,3072]{1,0:T(8,128)(2,1)} %q_ref.1, bf16[192,3072]{1,0:T(8,128)(2,1)} %k_ref.1, bf16[192,3072]{1,0:T(8,128)(2,1)} %v_ref.1, bf16[16,128]{1,0:T(8,128)(2,1)} %pad_bitcast_fusion.id_ref), custom_call_target="tpu_custom_call" | custom-call | tf_op jit(solution)/shard_map/pack/pallas_call | solution.py:41
  8.9 6.8 %all-to-all-start = ((bf16[16,1072,128]{2,1,0:T(8,128)(2,1)}), bf16[16,1072,128]{2,1,0:T(8,128)(2,1)}, u32[]{:S(2)}, u32[]{:S(2)}) async-start(bf16[16,1072,128]{2,1,0:T(8,128)(2,1)} %pack.1), calls=%async_computation | async-start | bytes 8781824 | tf_op jit(solution)/shard_map/all_to_all | solution.py:270
  15.8 79.6 %all-to-all-done.got = bf16[16,1072,128]{2,1,0:T(8,128)(2,1)} async-done(((bf16[16,1072,128]{2,1,0:T(8,128)(2,1)}), bf16[16,1072,128]{2,1,0:T(8,128)(2,1)}, u32[]{:S(2)}, u32[]{:S(2)}) %all-to-all-start) | async-done | bytes 4390944 | tf_op jit(solution)/shard_map/all_to_all | solution.py:270
  95.4 36.6 %attend.1 = bf16[16,576,128]{2,1,0:T(8,128)(2,1)} custom-call(s32[1]{0:T(128)} %bitcast.mp_ref, bf16[16,1072,128]{2,1,0:T(8,128)(2,1)} %all-to-all-done.got), custom_call_target="tpu_custom_call" | custom-call | tf_op jit(solution)/shard_map/attend/pallas_call | solution.py:150
  132.0 9.2 %all-to-all-start.1 = ((bf16[16,576,128]{2,1,0:T(8,128)(2,1)}), bf16[16,576,128]{2,1,0:T(8,128)(2,1)S(1)}, u32[]{:S(2)}, u32[]{:S(2)}) async-start(bf16[16,576,128]{2,1,0:T(8,128)(2,1)} %attend.1), calls=%async_computation.1 | async-start | bytes 4718592 | tf_op jit(solution)/shard_map/all_to_all | solution.py:272
  141.9 0.0 copy-done
  141.9 0.6 copy.12
  142.5 31.4 %all-to-all-done.1.got = bf16[16,576,128]{2,1,0:T(8,128)(2,1)S(1)} async-done(((bf16[16,576,128]{2,1,0:T(8,128)(2,1)}), bf16[16,576,128]{2,1,0:T(8,128)(2,1)S(1)}, u32[]{:S(2)}, u32[]{:S(2)}) %all-to-all-start.1) | async-done | bytes 2359328 | tf_op jit(solution)/shard_map/all_to_all | solution.py:272
  173.9 0.0 copy-start.1
  173.9 1.4 copy-done.1
  175.3 10.2 %project.1 = (bf16[384,1536]{1,0:T(8,128)(2,1)}, f32[384,1536]{1,0:T(8,128)}, f32[8,384]{1,0:T(8,128)}) custom-call(bf16[16,576,128]{2,1,0:T(8,128)(2,1)} %copy-done.1, bf16[3072,1536]{1,0:T(8,128)(2,1)} %w_ref.1, bf16[384,1536]{1,0:T(8,128)(2,1)} %res_ref.1, f32[3,1536]{1,0:T(4,128)} %bitcast.10), custom_call_target="tpu_custom_call" | custom-call | tf_op jit(solution)/shard_map/project/pallas_call | solution.py:212
  185.5 0.5 collective-permute-start
  186.0 3.8 %collective-permute-done.other_ref = f32[8,384]{1,0:T(8,128)S(1)} collective-permute-done((f32[8,384]{1,0:T(8,128)}, f32[8,384]{1,0:T(8,128)S(1)}, u32[]{:S(2)}, u32[]{:S(2)}) %collective-permute-start) | collective-permute-done | bytes 12320 | tf_op jit(solution)/shard_map/ppermute | solution.py:274
  189.8 0.0 copy-start.2
  189.8 0.6 copy-done.2
  190.4 2.8 %norm.1 = bf16[384,1536]{1,0:T(8,128)(2,1)} custom-call(f32[384,1536]{1,0:T(8,128)} %get-tuple-element.6.stream_ref, f32[8,384]{1,0:T(8,128)} %get-tuple-element.7.mine_ref, f32[8,384]{1,0:T(8,128)} %copy-done.2, f32[3,1536]{1,0:T(4,128)} %bitcast.11), custom_call_target="tpu_custom_call" | custom-call | tf_op jit(solution)/shard_map/norm/pallas_call | solution.py:255
  (1 shorter events, 0.0 us)
Async XLA Ops:
  0.6 141.2 %copy-start = (f32[50,3,1536]{2,0,1:T(8,128)S(1)}, f32[50,3,1536]{2,0,1:T(8,128)}, u32[]{:S(2)}) copy-start(f32[50,3,1536]{2,0,1:T(8,128)} %param.14) | copy-start | bytes 2764804
  8.9 86.4 %all-to-all-start = ((bf16[16,1072,128]{2,1,0:T(8,128)(2,1)}), bf16[16,1072,128]{2,1,0:T(8,128)(2,1)}, u32[]{:S(2)}, u32[]{:S(2)}) async-start(bf16[16,1072,128]{2,1,0:T(8,128)(2,1)} %pack.1), calls=%async_computation | async-start | bytes 8781824 | tf_op jit(solution)/shard_map/all_to_all | solution.py:270
  132.0 41.9 %all-to-all-start.1 = ((bf16[16,576,128]{2,1,0:T(8,128)(2,1)}), bf16[16,576,128]{2,1,0:T(8,128)(2,1)S(1)}, u32[]{:S(2)}, u32[]{:S(2)}) async-start(bf16[16,576,128]{2,1,0:T(8,128)(2,1)} %attend.1), calls=%async_computation.1 | async-start | bytes 4718592 | tf_op jit(solution)/shard_map/all_to_all | solution.py:272
  173.9 1.4 copy-start.1
  185.5 4.3 %collective-permute-start = (f32[8,384]{1,0:T(8,128)}, f32[8,384]{1,0:T(8,128)S(1)}, u32[]{:S(2)}, u32[]{:S(2)}) collective-permute-start(f32[8,384]{1,0:T(8,128)} %get-tuple-element.7.mine_ref), channel_id=1, source_target_pairs={{0,1},{1,0},{2,3},{3,2},{4,5},{5,4},{6,7},{7,6},{8,9},{9,8},{10,11... | collective-permute-start | bytes 36872 | tf_op jit(solution)/shard_map/ppermute | solution.py:274
  189.8 0.6 copy-start.2

commit v2 on v1

--- a/solution.py
+++ b/solution.py
@@ -267,8 +267,11 @@
     mod_rows = lax.dynamic_index_in_dim(modulation, timestep[0], 0, keepdims=False)
     spare = jnp.full(((SENT - ID) * HEAD_DIM - ROWS,), 7, jnp.int32)
     id_rows = jnp.concatenate([video_ids, spare]).reshape(SENT - ID, HEAD_DIM).astype(BF16)
-    got = lax.all_to_all(pack(queries, keys, values, id_rows), axes, 0, 0)
     mp_index = lax.axis_index("mp").astype(jnp.int32).reshape(1)
+    packed, mp_index, mod_rows = lax.optimization_barrier(
+        (pack(queries, keys, values, id_rows), mp_index, mod_rows)
+    )
+    got = lax.all_to_all(packed, axes, 0, 0)
     back = lax.all_to_all(attend(mp_index, got), axes, 0, 0)
     hidden, stream, mine = project(back, out_weight, residual, mod_rows)
     other = lax.ppermute(mine, "mp", [(0, 1), (1, 0)])

time: 196 us -> 160 us (0.82)
  the two profiles are of different devices: /device:TPU:41 before, /device:TPU:38 now
where the time goes in v2:
time: 160 us; the launch traced here: 158 us
  blocking collectives  92.5 us (58%)
  Pallas kernels  55.8 us (35%)
  waiting for transfers between devices  4.73 us (3%)
  local copies, waits for them, and re-layouts  1.82 us (1%)
    all_to_all x1, blocking collectives, local(): got = lax.all_to_all(packed, axes, 0, 0)  59 us
    pallas_call x1, Pallas kernels, attend(): pl.pallas_call(attend_kernel, grid=(SHARDS // 2,), in_specs=[pl.BlockSpec...  35.8 us
    all_to_all x1, blocking collectives, local(): back = lax.all_to_all(attend(mp_index, got), axes, 0, 0)  33.5 us
    pallas_call x1, Pallas kernels, project(): pl.pallas_call(project_kernel, grid=(cols // block,), in_specs=[pl.BlockS...  10.2 us
    pallas_call x1, Pallas kernels, pack(): pl.pallas_call(pack_kernel, grid=(SHARDS // 2,), in_specs=[heads3, heads3...  6.95 us
    ppermute x1, waiting for transfers between devices, local(): other = lax.ppermute(mine, 'mp', [(0, 1), (1, 0)])  4.73 us
  transfers between devices with their start and end apart: 1, of which 1 were waited for; matrix products, arithmetic and copies ran while one was open for 0% of the time, Pallas kernels for 0%

profile of v2, /device:TPU:38, one launch (start us, length us, event | category | flops | bytes accessed | tf_op | source)
XLA Modules:
  0.0 157.6 jit_solution(12513395743880435526)
XLA Ops:
  0.6 0.0 copy-start
  1.4 0.7 convert.4
  2.1 0.6 pad_bitcast_fusion.id_ref
  2.7 0.0 copy-done
  2.7 0.6 copy.12
  3.3 6.9 %pack.1 = bf16[16,1072,128]{2,1,0:T(8,128)(2,1)} custom-call(bf16[192,3072]{1,0:T(8,128)(2,1)} %q_ref.1, bf16[192,3072]{1,0:T(8,128)(2,1)} %k_ref.1, bf16[192,3072]{1,0:T(8,128)(2,1)} %v_ref.1, bf16[16,128]{1,0:T(8,128)(2,1)} %pad_bitcast_fusion.id_ref), custom_call_target="tpu_custom_call" | custom-call | tf_op jit(solution)/shard_map/pack/pallas_call | solution.py:41
  10.2 59.0 %all_to_all.10.got = bf16[16,1072,128]{2,1,0:T(8,128)(2,1)} all-to-all(bf16[16,1072,128]{2,1,0:T(8,128)(2,1)} %pack.1), channel_id=1, replica_groups=mesh['dp'=8,'seq'=8,'mp'=2] {'seq','mp'}, dimensions={0} | all-to-all | bytes 8781824 | tf_op jit(solution)/shard_map/all_to_all | solution.py:274
  69.2 35.8 %attend.1 = bf16[16,576,128]{2,1,0:T(8,128)(2,1)} custom-call(s32[1]{0:T(128)} %bitcast.1.mp_ref, bf16[16,1072,128]{2,1,0:T(8,128)(2,1)} %all_to_all.10.got), custom_call_target="tpu_custom_call" | custom-call | tf_op jit(solution)/shard_map/attend/pallas_call | solution.py:150
  105.0 33.5 %all_to_all.11.got = bf16[16,576,128]{2,1,0:T(8,128)(2,1)} all-to-all(bf16[16,576,128]{2,1,0:T(8,128)(2,1)} %attend.1), channel_id=1, replica_groups=mesh['dp'=8,'seq'=8,'mp'=2] {'seq','mp'}, dimensions={0} | all-to-all | bytes 4718592 | tf_op jit(solution)/shard_map/all_to_all | solution.py:275
  138.5 10.2 %project.1 = (bf16[384,1536]{1,0:T(8,128)(2,1)}, f32[384,1536]{1,0:T(8,128)}, f32[8,384]{1,0:T(8,128)}) custom-call(bf16[16,576,128]{2,1,0:T(8,128)(2,1)} %all_to_all.11.got, bf16[3072,1536]{1,0:T(8,128)(2,1)} %w_ref.1, bf16[384,1536]{1,0:T(8,128)(2,1)} %res_ref.1, f32[3,1536]{1,0:T(4,128)} %bitcast.10), custom_call_target="tpu_custom_call" | custom-call | tf_op jit(solution)/shard_map/project/pallas_call | solution.py:212
  148.8 0.7 collective-permute-start
  149.4 4.7 %collective-permute-done.other_ref = f32[8,384]{1,0:T(8,128)S(1)} collective-permute-done((f32[8,384]{1,0:T(8,128)}, f32[8,384]{1,0:T(8,128)S(1)}, u32[]{:S(2)}, u32[]{:S(2)}) %collective-permute-start) | collective-permute-done | bytes 12320 | tf_op jit(solution)/shard_map/ppermute | solution.py:277
  154.2 0.0 copy-start.1
  154.2 0.6 copy-done.1
  154.8 2.8 %norm.1 = bf16[384,1536]{1,0:T(8,128)(2,1)} custom-call(f32[384,1536]{1,0:T(8,128)} %get-tuple-element.12.stream_ref, f32[8,384]{1,0:T(8,128)} %get-tuple-element.13.mine_ref, f32[8,384]{1,0:T(8,128)} %copy-done.1, f32[3,1536]{1,0:T(4,128)} %bitcast.11), custom_call_target="tpu_custom_call" | custom-call | tf_op jit(solution)/shard_map/norm/pallas_call | solution.py:255
  (1 shorter events, 0.0 us)
Async XLA Ops:
  0.6 2.0 %copy-start = (f32[50,3,1536]{2,0,1:T(8,128)S(1)}, f32[50,3,1536]{2,0,1:T(8,128)}, u32[]{:S(2)}) copy-start(f32[50,3,1536]{2,0,1:T(8,128)} %param.14) | copy-start | bytes 2764804
  148.8 5.4 %collective-permute-start = (f32[8,384]{1,0:T(8,128)}, f32[8,384]{1,0:T(8,128)S(1)}, u32[]{:S(2)}, u32[]{:S(2)}) collective-permute-start(f32[8,384]{1,0:T(8,128)} %get-tuple-element.13.mine_ref), channel_id=1, source_target_pairs={{0,1},{1,0},{2,3},{3,2},{4,5},{5,4},{6,7},{7,6},{8,9},{9,8},{10,11... | collective-permute-start | bytes 36872 | tf_op jit(solution)/shard_map/ppermute | solution.py:277
  154.2 0.6 copy-start.1

commit v3 on v2

v3 whole, which is shorter than its diff:
```python
import functools
import math

import jax
import jax.numpy as jnp
from jax import lax
from jax.experimental import pallas as pl
from jax.experimental.pallas import tpu as pltpu
from jax.sharding import PartitionSpec as P

HEAD_DIM = 128
SHARDS = 16
ROWS = 192
HALF = ROWS // 2
TOKENS = SHARDS * ROWS
QF, KF, KM, VF, VM, QM, ID = 0, 192, 384, 576, 768, 960, 1056
SENT = 1072
BACK = 3 * ROWS
TILE = 512
SPARE = -(-TILE // ROWS)
BIG = 32768.0
SCALE = math.log2(math.e) / math.sqrt(HEAD_DIM)
F32 = jnp.float32
BF16 = jnp.bfloat16


def pieces(s, m):
    full, mid = 3 * s + 2 * m, 3 * s + 1
    return (
        (0, QF, ROWS, 0, full),
        (1, KF, ROWS, 0, full),
        (1, KM, ROWS, 0, mid),
        (2, VF, ROWS, 0, full),
        (2, VM, ROWS, 0, mid),
        (0, QM, HALF, m * HALF, mid),
    )


def pack_kernel(q_ref, k_ref, v_ref, id_ref, out_ref, sem):
    given = (q_ref, k_ref, v_ref)
    for s in range(SHARDS // 2):
        for m in range(2):
            for which, to, count, row, head in pieces(s, m):
                source = given[which].at[pl.ds(row, count), pl.ds(head * HEAD_DIM, HEAD_DIM)]
                pltpu.make_async_copy(source, out_ref.at[2 * s + m, pl.ds(to, count)], sem).start()
            pltpu.make_async_copy(id_ref, out_ref.at[2 * s + m, pl.ds(ID, SENT - ID)], sem).start()
    pltpu.make_async_copy(out_ref, out_ref, sem).wait()


def pack(queries, keys, values, id_rows):
    anywhere = pl.BlockSpec(memory_space=pl.ANY)
    return pl.pallas_call(
        pack_kernel,
        in_specs=[anywhere] * 4,
        out_specs=pl.BlockSpec(memory_space=pltpu.VMEM),
        out_shape=pltpu.VMEM((SHARDS, SENT, HEAD_DIM), BF16),
        scratch_shapes=[pltpu.SemaphoreType.DMA],
        compiler_params=pltpu.CompilerParams(vmem_limit_bytes=1 << 20),
        name="pack",
    )(queries, keys, values, id_rows)


def attend_kernel(mp_ref, got, out_ref, qf, qm, kf, km, vf, vm, ids, is_q, is_m, is_k, score, peak, top, acc, bounds, sem):
    copies = []
    for n, (first, count, ref) in enumerate(
        (
            (ID, SENT - ID, ids),
            (QF, ROWS, qf),
            (QM, HALF, qm),
            (KF, ROWS, kf),
            (KM, ROWS, km),
            (VF, ROWS, vf),
            (VM, ROWS, vm),
        )
    ):
        copy = pltpu.make_async_copy(got.at[:, pl.ds(first, count)], ref.at[pl.ds(0, SHARDS)], sem.at[n])
        copy.start()
        copies.append(copy)
    for ref in (kf, km, vf, vm):
        ref[SHARDS:] = jnp.zeros((SPARE, ROWS, HEAD_DIM), BF16)
    acc[...] = jnp.zeros_like(acc)
    top[...] = jnp.zeros_like(top)
    copies[0].wait()
    every = ids[...].astype(F32)
    for v in range(3):
        bounds[v] = jnp.sum((every <= v + 0.5).astype(F32)).astype(jnp.int32)
    c0, c1, c2 = bounds[0], bounds[1], bounds[2]
    lane = lax.broadcasted_iota(jnp.int32, (1, HEAD_DIM), 1)
    low_of = jnp.where(lane == 1, c0, jnp.where(lane == 2, c1, jnp.where(lane == 3, c2, 0)))
    end = TOKENS + SPARE * ROWS
    high_of = jnp.where(lane == 0, c0, jnp.where(lane == 1, c1, jnp.where(lane == 2, c2, jnp.where(lane == 3, TOKENS, end))))

    def inside(first, count):
        token = lax.broadcasted_iota(jnp.int32, (count, HEAD_DIM), 0) + first
        return (token >= low_of) & (token < high_of)

    def fill(b, _):
        here = inside(b * ROWS, ROWS)
        is_k[b] = jnp.where(here, 0.0, -BIG).astype(BF16)
        is_q[b] = jnp.where(here, 1.0, 0.0).astype(BF16)
        is_m[b] = jnp.where(inside(b * ROWS + mp_ref[0] * HALF, HALF), 1.0, 0.0).astype(BF16)
        return 0

    lax.fori_loop(0, SHARDS, fill, 0)
    for b in range(SHARDS, SHARDS + SPARE):
        is_k[b] = jnp.where(inside(b * ROWS, ROWS), 0.0, -BIG).astype(BF16)
    for copy in copies[1:]:
        copy.wait()

    def span(t):
        first = t * (2 * ROWS)
        last = first + (2 * ROWS - 1)
        low = jnp.where(first >= c2, c2, jnp.where(first >= c1, c1, jnp.where(first >= c0, c0, 0)))
        high = jnp.where(last < c0, c0, jnp.where(last < c1, c1, jnp.where(last < c2, c2, TOKENS)))
        low = (low // 16) * 16
        return low, (high - low + TILE - 1) // TILE

    def flat(ref):
        return ref.reshape(ref.shape[0] * ref.shape[1], HEAD_DIM)

    parts = ((slice(0, 2 * ROWS), qf, is_q, kf, vf), (slice(2 * ROWS, BACK), qm, is_m, km, vm))

    def look(t, key, slot):
        at = pl.ds(pl.multiple_of(key, 16), TILE)
        same = flat(is_k)[at, :]
        for rows, q_ref, is_ref, k_ref, _ in parts:
            count = rows.stop - rows.start
            mine = pl.ds(pl.multiple_of(t * count, count), count)
            q = jnp.concatenate([flat(q_ref)[mine, :], flat(is_ref)[mine, :]], axis=1)
            k = jnp.concatenate([flat(k_ref)[at, :], same], axis=1)
            found = lax.dot_general(q, k, (((1,), (1,)), ((), ())), preferred_element_type=F32)
            score[slot, rows] = found
            peak[slot, rows] = jnp.broadcast_to(jnp.max(found, axis=1, keepdims=True), (count, HEAD_DIM))

    def step(carry, slot):
        t, i = carry
        low, steps = span(t)
        done = i + 1 == steps
        next_t = jnp.where(done, t + 1, t)
        next_i = jnp.where(done, 0, i + 1)
        look_t = jnp.minimum(next_t, SHARDS // 2 - 1)
        look(look_t, span(look_t)[0] + next_i * TILE, 1 - slot)
        at = pl.ds(pl.multiple_of(low + i * TILE, 16), TILE)
        ones = jnp.ones((TILE, HEAD_DIM), BF16)
        for rows, _, _, _, v_ref in parts:
            old = jnp.where(i == 0, -1e30, top[rows])
            new = jnp.maximum(old, peak[slot, rows])
            top[rows] = new
            kept = jnp.exp2((old - new) * SCALE)
            weight = jnp.concatenate(
                [
                    jnp.exp2((score[slot, rows, c : c + HEAD_DIM] - new) * SCALE).astype(BF16)
                    for c in range(0, TILE, HEAD_DIM)
                ],
                axis=1,
            )
            v = jnp.concatenate([flat(v_ref)[at, :], ones], axis=1)
            more = jnp.dot(weight, v, preferred_element_type=F32)
            acc[rows] = acc[rows] * jnp.concatenate([kept, kept], axis=1) + more

        @pl.when(done & (t < SHARDS // 2))
        def _():
            result = (acc[:, :HEAD_DIM] / acc[:, HEAD_DIM:]).astype(BF16)
            out_ref[2 * t] = result
            out_ref[2 * t + 1] = result

        return next_t, next_i

    total = sum(span(t)[1] for t in range(SHARDS // 2))
    look(0, 0, 0)
    lax.fori_loop(0, (total + 1) // 2, lambda _, carry: step(step(carry, 0), 1), (0, 0))


def attend(mp_index, got):
    rows = lambda n, spare: pltpu.VMEM((SHARDS + spare, n, HEAD_DIM), BF16)
    return pl.pallas_call(
        attend_kernel,
        in_specs=[pl.BlockSpec(memory_space=pltpu.SMEM), pl.BlockSpec(memory_space=pl.ANY)],
        out_shape=jax.ShapeDtypeStruct((SHARDS, BACK, HEAD_DIM), BF16),
        scratch_shapes=[
            rows(ROWS, 0),
            rows(HALF, 0),
            rows(ROWS, SPARE),
            rows(ROWS, SPARE),
            rows(ROWS, SPARE),
            rows(ROWS, SPARE),
            rows(SENT - ID, 0),
            rows(ROWS, 0),
            rows(HALF, 0),
            rows(ROWS, SPARE),
            pltpu.VMEM((2, BACK, TILE), F32),
            pltpu.VMEM((2, BACK, HEAD_DIM), F32),
            pltpu.VMEM((BACK, HEAD_DIM), F32),
            pltpu.VMEM((BACK, 2 * HEAD_DIM), F32),
            pltpu.SMEM((4,), jnp.int32),
            pltpu.SemaphoreType.DMA((7,)),
        ],
        compiler_params=pltpu.CompilerParams(vmem_limit_bytes=20 << 20),
        name="attend",
    )(mp_index, got)


def project_kernel(got, w_ref, res_ref, mod_ref, hidden_ref, stream_ref, stat_ref, attended, sums):
    j = pl.program_id(0)

    @pl.when(j == 0)
    def _():
        for s in range(SHARDS // 2):
            mid = slice((3 * s + 1) * HEAD_DIM, (3 * s + 2) * HEAD_DIM)
            for m in range(2):
                full = slice((3 * s + 2 * m) * HEAD_DIM, (3 * s + 2 * m + 1) * HEAD_DIM)
                d = 2 * s + m
                attended[:, full] = got[d, : 2 * ROWS]
                for b in range(2):
                    attended[b * ROWS + m * HALF : b * ROWS + (m + 1) * HALF, mid] = got[
                        d, 2 * ROWS + b * HALF : 2 * ROWS + (b + 1) * HALF
                    ]
        sums[...] = jnp.zeros_like(sums)

    projected = jnp.dot(attended[...], w_ref[...], preferred_element_type=F32)
    stream = res_ref[...].astype(F32) + mod_ref[0:1, :] * projected
    hidden_ref[...] = stream.astype(BF16)
    stream_ref[...] = stream
    one, two = sums[0], sums[1]
    for c in range(stream.shape[1] // HEAD_DIM):
        part = stream[:, c * HEAD_DIM : (c + 1) * HEAD_DIM]
        one = one + part
        two = two + part * part
    sums[0] = one
    sums[1] = two

    @pl.when(j == pl.num_programs(0) - 1)
    def _():
        stat_ref[...] = jnp.zeros_like(stat_ref)
        stat_ref[0:1, :] = jnp.sum(sums[0].T, axis=0, keepdims=True)
        stat_ref[1:2, :] = jnp.sum(sums[1].T, axis=0, keepdims=True)


def project(got, out_weight, residual, mod_rows):
    width, cols = out_weight.shape
    rows = residual.shape[0]
    block = 512
    column = lambda j: (0, j)
    return pl.pallas_call(
        project_kernel,
        grid=(cols // block,),
        in_specs=[
            pl.BlockSpec((SHARDS, BACK, HEAD_DIM), lambda j: (0, 0, 0)),
            pl.BlockSpec((width, block), column),
            pl.BlockSpec((rows, block), column),
            pl.BlockSpec((3, block), column),
        ],
        out_specs=[
            pl.BlockSpec((rows, block), column),
            pl.BlockSpec((rows, block), column),
            pl.BlockSpec((8, rows), lambda j: (0, 0)),
        ],
        out_shape=[
            jax.ShapeDtypeStruct((rows, cols), BF16),
            jax.ShapeDtypeStruct((rows, cols), F32),
            jax.ShapeDtypeStruct((8, rows), F32),
        ],
        scratch_shapes=[pltpu.VMEM((rows, width), BF16), pltpu.VMEM((2, rows, HEAD_DIM), F32)],
        compiler_params=pltpu.CompilerParams(vmem_limit_bytes=24 << 20),
        name="project",
    )(got, out_weight, residual, mod_rows)


def norm_kernel(width, stream_ref, mine_ref, other_ref, mod_ref, out_ref):
    stats = mine_ref[...] + other_ref[...]
    mean = stats[0:1, :] / width
    var = stats[1:2, :] / width - mean * mean
    rows = mean.shape[1]
    mean = jnp.broadcast_to(mean, (HEAD_DIM, rows)).T
    inv = jnp.broadcast_to(lax.rsqrt(var + 1e-06), (HEAD_DIM, rows)).T
    for c in range(stream_ref.shape[1] // HEAD_DIM):
        at = slice(c * HEAD_DIM, (c + 1) * HEAD_DIM)
        shift = mod_ref[1:2, at]
        scale = mod_ref[2:3, at]
        out_ref[:, at] = ((stream_ref[:, at] - mean) * inv * (1.0 + scale) + shift).astype(BF16)


def norm(stream, mine, other, mod_rows, width):
    rows, cols = stream.shape
    block = 768
    column = lambda j: (0, j)
    whole = pl.BlockSpec((8, rows), lambda j: (0, 0))
    return pl.pallas_call(
        functools.partial(norm_kernel, width),
        grid=(cols // block,),
        in_specs=[pl.BlockSpec((rows, block), column), whole, whole, pl.BlockSpec((3, block), column)],
        out_specs=pl.BlockSpec((rows, block), column),
        out_shape=jax.ShapeDtypeStruct((rows, cols), BF16),
        compiler_params=pltpu.CompilerParams(vmem_limit_bytes=12 << 20),
        name="norm",
    )(stream, mine, other, mod_rows)


def local(residual, queries, keys, values, video_ids, timestep, modulation, out_weight):
    axes = ("seq", "mp")
    mod_rows = lax.dynamic_index_in_dim(modulation, timestep[0], 0, keepdims=False)
    spare = jnp.full(((SENT - ID) * HEAD_DIM - ROWS,), 7, jnp.int32)
    id_rows = jnp.concatenate([video_ids, spare]).reshape(SENT - ID, HEAD_DIM).astype(BF16)
    mp_index = lax.axis_index("mp").astype(jnp.int32).reshape(1)
    packed, mp_index, mod_rows = lax.optimization_barrier(
        (pack(queries, keys, values, id_rows), mp_index, mod_rows)
    )
    got = lax.all_to_all(packed, axes, 0, 0)
    back = lax.all_to_all(attend(mp_index, got), axes, 0, 0)
    hidden, stream, mine = project(back, out_weight, residual, mod_rows)
    other = lax.ppermute(mine, "mp", [(0, 1), (1, 0)])
    return hidden, norm(stream, mine, other, mod_rows, queries.shape[1])


def solution(mesh):
    return jax.shard_map(
        local,
        mesh=mesh,
        in_specs=(
            P(("dp", "seq"), "mp"),
            P(("dp", "seq", "mp"), None),
            P(("dp", "seq", "mp"), None),
            P(("dp", "seq", "mp"), None),
            P(("dp", "seq", "mp")),
            P("dp"),
            P(None, None, "mp"),
            P(None, "mp"),
        ),
        out_specs=(P(("dp", "seq"), "mp"), P(("dp", "seq"), "mp")),
        check_vma=False,
    )
```

time: 160 us -> 134 us (0.84)
  the two profiles are of different devices: /device:TPU:38 before, /device:TPU:64 now
where the time goes in v3:
time: 134 us; the launch traced here: 131 us
  blocking collectives  95.8 us (71%)
  Pallas kernels  24.4 us (18%)
  waiting for transfers between devices  4.41 us (3%)
  local copies, waits for them, and re-layouts  3.87 us (3%)
  between operations  1.47 us (1%)
    all_to_all x1, blocking collectives, local(): got = lax.all_to_all(packed, axes, 0, 0)  60.8 us
    all_to_all x1, blocking collectives, local(): back = lax.all_to_all(attend(mp_index, got), axes, 0, 0)  35 us
    pallas_call x1, Pallas kernels, attend(): pl.pallas_call(attend_kernel, in_specs=[pl.BlockSpec(memory_space=pltpu.S...  14.7 us
    pallas_call x1, Pallas kernels, project(): pl.pallas_call(project_kernel, grid=(cols // block,), in_specs=[pl.BlockS...  6.84 us
    ppermute x1, waiting for transfers between devices, local(): other = lax.ppermute(mine, 'mp', [(0, 1), (1, 0)])  4.41 us
    unnamed x17, local copies, waits for them, and re-layouts  3.85 us
  transfers between devices with their start and end apart: 1, of which 1 were waited for; matrix products, arithmetic and copies ran while one was open for 0% of the time, Pallas kernels for 0%

profile of v3, /device:TPU:64, one launch (start us, length us, event | category | flops | bytes accessed | tf_op | source)
XLA Modules:
  0.0 131.5 jit_solution(9614153443828236235)
XLA Ops:
  0.6 0.0 copy-start
  1.4 0.7 convert.4
  2.1 0.0 copy-done
  2.1 0.0 copy-start.1
  2.1 1.3 copy-done.1
  3.4 0.0 copy-start.2
  3.4 1.3 copy-done.2
  4.7 0.0 copy-start.3
  4.7 1.3 copy-done.3
  5.9 1.3 pack.1
  7.2 0.0 slice-start
  7.2 0.0 slice-start.1
  7.2 60.8 %all_to_all.10.got = bf16[16,1072,128]{2,1,0:T(8,128)(2,1)S(1)} all-to-all(bf16[16,1072,128]{2,1,0:T(8,128)(2,1)S(1)} %pack.1), channel_id=1, replica_groups=mesh['dp'=8,'seq'=8,'mp'=2] {'seq','mp'}, dimensions={0} | all-to-all | bytes 8781824 | tf_op jit(solution)/shard_map/all_to_all | solution.py:308
  68.1 14.7 %attend.1 = bf16[16,576,128]{2,1,0:T(8,128)(2,1)S(1)} custom-call(s32[1]{0:T(128)} %bitcast.1.mp_ref, bf16[16,1072,128]{2,1,0:T(8,128)(2,1)S(1)} %all_to_all.10.got), custom_call_target="tpu_custom_call" | custom-call | tf_op jit(solution)/shard_map/attend/pallas_call | solution.py:176
  82.8 0.0 copy-start.4
  82.8 35.0 %all_to_all.11.got = bf16[16,576,128]{2,1,0:T(8,128)(2,1)S(1)} all-to-all(bf16[16,576,128]{2,1,0:T(8,128)(2,1)S(1)} %attend.1), channel_id=1, replica_groups=mesh['dp'=8,'seq'=8,'mp'=2] {'seq','mp'}, dimensions={0} | all-to-all | bytes 4718592 | tf_op jit(solution)/shard_map/all_to_all | solution.py:309
  117.8 0.0 slice-done
  117.8 0.0 slice-done.1
  117.8 0.0 slice-done.2
  117.8 0.0 copy-done.4
  117.8 6.8 %project.1 = (bf16[384,1536]{1,0:T(8,128)(2,1)}, f32[384,1536]{1,0:T(8,128)S(1)}, f32[8,384]{1,0:T(8,128)S(1)}) custom-call(bf16[16,576,128]{2,1,0:T(8,128)(2,1)S(1)} %all_to_all.11.got, bf16[3072,1536]{1,0:T(8,128)(2,1)S(1)} %bitcast.11, bf16[384,1536]{1,0:T(8,128)(2,1)S(1)} %copy-done.4, f32[3,1536]{1,0:T(4,128)S(1)} %bitcast.12), custom_call_target="tpu_custom_call" | custom-call | tf_op jit(solution)/shard_map/project/pallas_call | solution.py:244
  124.6 0.8 collective-permute-start
  125.4 4.4 %collective-permute-done.other_ref = f32[8,384]{1,0:T(8,128)S(1)} collective-permute-done((f32[8,384]{1,0:T(8,128)S(1)}, f32[8,384]{1,0:T(8,128)S(1)}, u32[]{:S(2)}, u32[]{:S(2)}) %collective-permute-start) | collective-permute-done | bytes 12320 | tf_op jit(solution)/shard_map/ppermute | solution.py:311
  129.8 1.6 %norm.1 = bf16[384,1536]{1,0:T(8,128)(2,1)} custom-call(f32[384,1536]{1,0:T(8,128)S(1)} %get-tuple-element.12.stream_ref, f32[8,384]{1,0:T(8,128)S(1)} %get-tuple-element.13.mine_ref, f32[8,384]{1,0:T(8,128)S(1)} %collective-permute-done.other_ref, f32[3,1536]{1,0:T(4,128)S(1)} %bitcast.13), custom_call_target="tpu_custom_call" | custom-call | tf_op jit(solution)/shard_map/norm/pallas_call | solution.py:288
  (5 shorter events, 0.0 us)
Async XLA Ops:
  0.6 1.4 %copy-start = (f32[50,3,1536]{2,0,1:T(8,128)S(1)}, f32[50,3,1536]{2,0,1:T(8,128)}, u32[]{:S(2)}) copy-start(f32[50,3,1536]{2,0,1:T(8,128)} %param.14) | copy-start | bytes 2764804
  2.1 1.3 copy-start.1
  3.4 1.3 copy-start.2
  4.7 1.3 copy-start.3
  7.2 110.6 %slice-start = ((s8[9437184]{0:T(1024)(128)(4,1)}), s8[4194304]{0:T(1024)(128)(4,1)S(1)}, s32[]{:S(2)}) async-start(s8[9437184]{0:T(1024)(128)(4,1)} %bitcast.10), calls=%async_computation.2 | async-start | bytes 8388608
  7.2 110.5 %slice-start.1 = ((s8[9437184]{0:T(1024)(128)(4,1)}), s8[4194304]{0:T(1024)(128)(4,1)S(1)}, s32[]{:S(2)}) async-start(s8[9437184]{0:T(1024)(128)(4,1)} %bitcast.10), calls=%async_computation.3 | async-start | bytes 8388608
  68.1 49.7 %slice-start.2 = ((s8[9437184]{0:T(1024)(128)(4,1)}), s8[1048576]{0:T(1024)(128)(4,1)S(1)}, s32[]{:S(2)}) async-start(s8[9437184]{0:T(1024)(128)(4,1)} %bitcast.10), calls=%async_computation.4 | async-start | bytes 2097152
  82.8 35.0 %copy-start.4 = (bf16[384,1536]{1,0:T(8,128)(2,1)S(1)}, bf16[384,1536]{1,0:T(8,128)(2,1)}, u32[]{:S(2)}) copy-start(bf16[384,1536]{1,0:T(8,128)(2,1)} %res_ref.1) | copy-start | bytes 3538948
  124.6 5.2 %collective-permute-start = (f32[8,384]{1,0:T(8,128)S(1)}, f32[8,384]{1,0:T(8,128)S(1)}, u32[]{:S(2)}, u32[]{:S(2)}) collective-permute-start(f32[8,384]{1,0:T(8,128)S(1)} %get-tuple-element.13.mine_ref), channel_id=1, source_target_pairs={{0,1},{1,0},{2,3},{3,2},{4,5},{5,4},{6,7},{7,6},{8,9},{9,8},{10,11... | collective-permute-start | bytes 36872 | tf_op jit(solution)/shard_map/ppermute | solution.py:311

commit v4 on v3

--- a/solution.py
+++ b/solution.py
@@ -15,6 +15,7 @@
 TOKENS = SHARDS * ROWS
 QF, KF, KM, VF, VM, QM, ID = 0, 192, 384, 576, 768, 960, 1056
 SENT = 1072
+BLOCK = 512
 BACK = 3 * ROWS
 TILE = 512
 SPARE = -(-TILE // ROWS)
@@ -48,19 +49,18 @@
 
 
 def pack(queries, keys, values, id_rows):
-    anywhere = pl.BlockSpec(memory_space=pl.ANY)
     return pl.pallas_call(
         pack_kernel,
-        in_specs=[anywhere] * 4,
+        in_specs=[pl.BlockSpec(memory_space=pltpu.HBM)] * 3 + [pl.BlockSpec(memory_space=pl.ANY)],
         out_specs=pl.BlockSpec(memory_space=pltpu.VMEM),
         out_shape=pltpu.VMEM((SHARDS, SENT, HEAD_DIM), BF16),
         scratch_shapes=[pltpu.SemaphoreType.DMA],
         compiler_params=pltpu.CompilerParams(vmem_limit_bytes=1 << 20),
         name="pack",
-    )(queries, keys, values, id_rows)
-
-
-def attend_kernel(mp_ref, got, out_ref, qf, qm, kf, km, vf, vm, ids, is_q, is_m, is_k, score, peak, top, acc, bounds, sem):
+    )(*(pltpu.with_memory_space_constraint(x, pltpu.HBM) for x in (queries, keys, values)), id_rows)
+
+
+def attend_kernel(mp_ref, got, out_ref, qf, qm, kf, km, vf, vm, ids, is_q, is_m, is_k, score, peak, top, acc, bounds, spans, sem):
     copies = []
     for n, (first, count, ref) in enumerate(
         (
@@ -107,16 +107,22 @@
     for copy in copies[1:]:
         copy.wait()
 
-    def span(t):
+    for t in range(SHARDS // 2):
         first = t * (2 * ROWS)
         last = first + (2 * ROWS - 1)
         low = jnp.where(first >= c2, c2, jnp.where(first >= c1, c1, jnp.where(first >= c0, c0, 0)))
         high = jnp.where(last < c0, c0, jnp.where(last < c1, c1, jnp.where(last < c2, c2, TOKENS)))
         low = (low // 16) * 16
-        return low, (high - low + TILE - 1) // TILE
+        spans[0, t] = low
+        spans[1, t] = (high - low + TILE - 1) // TILE
+    spans[0, SHARDS // 2] = TOKENS
+    spans[1, SHARDS // 2] = 1
 
     def flat(ref):
         return ref.reshape(ref.shape[0] * ref.shape[1], HEAD_DIM)
+
+    def tile_of(t):
+        return jnp.minimum(t, SHARDS // 2 - 1)
 
     parts = ((slice(0, 2 * ROWS), qf, is_q, kf, vf), (slice(2 * ROWS, BACK), qm, is_m, km, vm))
 
@@ -125,25 +131,27 @@
         same = flat(is_k)[at, :]
         for rows, q_ref, is_ref, k_ref, _ in parts:
             count = rows.stop - rows.start
-            mine = pl.ds(pl.multiple_of(t * count, count), count)
+            mine = pl.ds(pl.multiple_of(tile_of(t) * count, count), count)
             q = jnp.concatenate([flat(q_ref)[mine, :], flat(is_ref)[mine, :]], axis=1)
             k = jnp.concatenate([flat(k_ref)[at, :], same], axis=1)
             found = lax.dot_general(q, k, (((1,), (1,)), ((), ())), preferred_element_type=F32)
             score[slot, rows] = found
             peak[slot, rows] = jnp.broadcast_to(jnp.max(found, axis=1, keepdims=True), (count, HEAD_DIM))
 
+    def after(t, i):
+        done = i + 1 == spans[1, t]
+        t = jnp.where(done, jnp.minimum(t + 1, SHARDS // 2), t)
+        i = jnp.where(done, 0, i + 1)
+        return t, i, spans[0, t] + i * TILE
+
     def step(carry, slot):
-        t, i = carry
-        low, steps = span(t)
-        done = i + 1 == steps
-        next_t = jnp.where(done, t + 1, t)
-        next_i = jnp.where(done, 0, i + 1)
-        look_t = jnp.minimum(next_t, SHARDS // 2 - 1)
-        look(look_t, span(look_t)[0] + next_i * TILE, 1 - slot)
-        at = pl.ds(pl.multiple_of(low + i * TILE, 16), TILE)
+        (t, i, key), (next_t, next_i, next_key) = carry
+        look(next_t, next_key, 1 - slot)
+        at = pl.ds(pl.multiple_of(key, 16), TILE)
+        start = (i == 0) & (t < SHARDS // 2)
         ones = jnp.ones((TILE, HEAD_DIM), BF16)
         for rows, _, _, _, v_ref in parts:
-            old = jnp.where(i == 0, -1e30, top[rows])
+            old = jnp.where(start, -1e30, top[rows])
             new = jnp.maximum(old, peak[slot, rows])
             top[rows] = new
             kept = jnp.exp2((old - new) * SCALE)
@@ -156,19 +164,17 @@
             )
             v = jnp.concatenate([flat(v_ref)[at, :], ones], axis=1)
             more = jnp.dot(weight, v, preferred_element_type=F32)
-            acc[rows] = acc[rows] * jnp.concatenate([kept, kept], axis=1) + more
-
-        @pl.when(done & (t < SHARDS // 2))
-        def _():
-            result = (acc[:, :HEAD_DIM] / acc[:, HEAD_DIM:]).astype(BF16)
-            out_ref[2 * t] = result
-            out_ref[2 * t + 1] = result
-
-        return next_t, next_i
-
-    total = sum(span(t)[1] for t in range(SHARDS // 2))
-    look(0, 0, 0)
-    lax.fori_loop(0, (total + 1) // 2, lambda _, carry: step(step(carry, 0), 1), (0, 0))
+            summed = acc[rows] * jnp.concatenate([kept, kept], axis=1) + more
+            acc[rows] = summed
+            result = (summed[:, :HEAD_DIM] / summed[:, HEAD_DIM:]).astype(BF16)
+            out_ref[2 * tile_of(t), rows] = result
+            out_ref[2 * tile_of(t) + 1, rows] = result
+        return (next_t, next_i, next_key), after(next_t, next_i)
+
+    total = sum(spans[1, t] for t in range(SHARDS // 2))
+    begin = (0, 0, spans[0, 0])
+    look(0, spans[0, 0], 0)
+    lax.fori_loop(0, (total + 1) // 2, lambda _, carry: step(step(carry, 0), 1), (begin, after(0, 0)))
 
 
 def attend(mp_index, got):
@@ -193,6 +199,7 @@
             pltpu.VMEM((BACK, HEAD_DIM), F32),
             pltpu.VMEM((BACK, 2 * HEAD_DIM), F32),
             pltpu.SMEM((4,), jnp.int32),
+            pltpu.SMEM((2, SHARDS // 2 + 1), jnp.int32),
             pltpu.SemaphoreType.DMA((7,)),
         ],
         compiler_params=pltpu.CompilerParams(vmem_limit_bytes=20 << 20),
@@ -200,67 +207,64 @@
     )(mp_index, got)
 
 
-def project_kernel(got, w_ref, res_ref, mod_ref, hidden_ref, stream_ref, stat_ref, attended, sums):
-    j = pl.program_id(0)
-
-    @pl.when(j == 0)
-    def _():
-        for s in range(SHARDS // 2):
-            mid = slice((3 * s + 1) * HEAD_DIM, (3 * s + 2) * HEAD_DIM)
-            for m in range(2):
-                full = slice((3 * s + 2 * m) * HEAD_DIM, (3 * s + 2 * m + 1) * HEAD_DIM)
-                d = 2 * s + m
-                attended[:, full] = got[d, : 2 * ROWS]
-                for b in range(2):
-                    attended[b * ROWS + m * HALF : b * ROWS + (m + 1) * HALF, mid] = got[
-                        d, 2 * ROWS + b * HALF : 2 * ROWS + (b + 1) * HALF
-                    ]
-        sums[...] = jnp.zeros_like(sums)
-
-    projected = jnp.dot(attended[...], w_ref[...], preferred_element_type=F32)
-    stream = res_ref[...].astype(F32) + mod_ref[0:1, :] * projected
-    hidden_ref[...] = stream.astype(BF16)
-    stream_ref[...] = stream
-    one, two = sums[0], sums[1]
-    for c in range(stream.shape[1] // HEAD_DIM):
-        part = stream[:, c * HEAD_DIM : (c + 1) * HEAD_DIM]
-        one = one + part
-        two = two + part * part
-    sums[0] = one
-    sums[1] = two
-
-    @pl.when(j == pl.num_programs(0) - 1)
-    def _():
-        stat_ref[...] = jnp.zeros_like(stat_ref)
-        stat_ref[0:1, :] = jnp.sum(sums[0].T, axis=0, keepdims=True)
-        stat_ref[1:2, :] = jnp.sum(sums[1].T, axis=0, keepdims=True)
+def project_kernel(got, w_ref, res_ref, mod_ref, hidden_hbm, stream_ref, stat_ref, attended, hidden, sums, sem):
+    for s in range(SHARDS // 2):
+        mid = slice((3 * s + 1) * HEAD_DIM, (3 * s + 2) * HEAD_DIM)
+        for m in range(2):
+            full = slice((3 * s + 2 * m) * HEAD_DIM, (3 * s + 2 * m + 1) * HEAD_DIM)
+            d = 2 * s + m
+            attended[:, full] = got[d, : 2 * ROWS]
+            for b in range(2):
+                attended[b * ROWS + m * HALF : b * ROWS + (m + 1) * HALF, mid] = got[
+                    d, 2 * ROWS + b * HALF : 2 * ROWS + (b + 1) * HALF
+                ]
+    sums[...] = jnp.zeros_like(sums)
+
+    def body(j, _):
+        block = pl.ds(pl.multiple_of(j * BLOCK, BLOCK), BLOCK)
+        projected = jnp.dot(attended[...], w_ref[:, block], preferred_element_type=F32)
+        stream = res_ref[:, block].astype(F32) + mod_ref[0:1, block] * projected
+        hidden[:, block] = stream.astype(BF16)
+        stream_ref[:, block] = stream
+        pltpu.make_async_copy(hidden.at[:, block], hidden_hbm.at[:, block], sem.at[j]).start()
+        one, two = sums[0], sums[1]
+        for c in range(0, BLOCK, HEAD_DIM):
+            part = stream[:, c : c + HEAD_DIM]
+            one = one + part
+            two = two + part * part
+        sums[0] = one
+        sums[1] = two
+        return 0
+
+    blocks = w_ref.shape[1] // BLOCK
+    lax.fori_loop(0, blocks, body, 0)
+    stat_ref[...] = jnp.zeros_like(stat_ref)
+    stat_ref[0:1, :] = jnp.sum(sums[0].T, axis=0, keepdims=True)
+    stat_ref[1:2, :] = jnp.sum(sums[1].T, axis=0, keepdims=True)
+    for j in range(blocks):
+        at = pl.ds(j * BLOCK, BLOCK)
+        pltpu.make_async_copy(hidden.at[:, at], hidden_hbm.at[:, at], sem.at[j]).wait()
 
 
 def project(got, out_weight, residual, mod_rows):
     width, cols = out_weight.shape
     rows = residual.shape[0]
-    block = 512
-    column = lambda j: (0, j)
+    whole = pl.BlockSpec(memory_space=pltpu.VMEM)
     return pl.pallas_call(
         project_kernel,
-        grid=(cols // block,),
-        in_specs=[
-            pl.BlockSpec((SHARDS, BACK, HEAD_DIM), lambda j: (0, 0, 0)),
-            pl.BlockSpec((width, block), column),
-            pl.BlockSpec((rows, block), column),
-            pl.BlockSpec((3, block), column),
-        ],
-        out_specs=[
-            pl.BlockSpec((rows, block), column),
-            pl.BlockSpec((rows, block), column),
-            pl.BlockSpec((8, rows), lambda j: (0, 0)),
-        ],
+        in_specs=[whole] * 4,
+        out_specs=[pl.BlockSpec(memory_space=pl.ANY), whole, whole],
         out_shape=[
             jax.ShapeDtypeStruct((rows, cols), BF16),
             jax.ShapeDtypeStruct((rows, cols), F32),
             jax.ShapeDtypeStruct((8, rows), F32),
         ],
-        scratch_shapes=[pltpu.VMEM((rows, width), BF16), pltpu.VMEM((2, rows, HEAD_DIM), F32)],
+        scratch_shapes=[
+            pltpu.VMEM((rows, width), BF16),
+            pltpu.VMEM((rows, cols), BF16),
+            pltpu.VMEM((2, rows, HEAD_DIM), F32),
+            pltpu.SemaphoreType.DMA((cols // BLOCK,)),
+        ],
         compiler_params=pltpu.CompilerParams(vmem_limit_bytes=24 << 20),
         name="project",
     )(got, out_weight, residual, mod_rows)

time: 134 us -> 128 us (0.955)
  the two profiles are of different devices: /device:TPU:64 before, /device:TPU:38 now
where the time goes in v4:
time: 128 us; the launch traced here: 127 us
  blocking collectives  95 us (74%)
  Pallas kernels  24.6 us (19%)
  waiting for transfers between devices  4.7 us (4%)
  between operations  1.46 us (1%)
    all_to_all x1, blocking collectives, local(): got = lax.all_to_all(packed, axes, 0, 0)  58.9 us
    all_to_all x1, blocking collectives, local(): back = lax.all_to_all(attend(mp_index, got), axes, 0, 0)  36.1 us
    pallas_call x1, Pallas kernels, attend(): pl.pallas_call(attend_kernel, in_specs=[pl.BlockSpec(memory_space=pltpu.S...  14.6 us
    pallas_call x1, Pallas kernels, project(): pl.pallas_call(project_kernel, in_specs=[whole] * 4, out_specs=[pl.BlockS...  5.9 us
    ppermute x1, waiting for transfers between devices, local(): other = lax.ppermute(mine, 'mp', [(0, 1), (1, 0)])  4.7 us
  transfers between devices with their start and end apart: 1, of which 1 were waited for; matrix products, arithmetic and copies ran while one was open for 0% of the time, Pallas kernels for 0%

profile of v4, /device:TPU:38, one launch (start us, length us, event | category | flops | bytes accessed | tf_op | source)
XLA Modules:
  0.0 127.0 jit_solution(8765182705527421364)
XLA Ops:
  0.6 0.0 copy-start
  1.4 0.7 convert.4
  2.1 0.0 copy-done
  2.1 2.4 %pack.1 = bf16[16,1072,128]{2,1,0:T(8,128)(2,1)S(1)} custom-call(bf16[192,3072]{1,0:T(8,128)(2,1)} %q_ref.1, bf16[192,3072]{1,0:T(8,128)(2,1)} %k_ref.1, bf16[192,3072]{1,0:T(8,128)(2,1)} %v_ref.1, bf16[16,128]{1,0:T(8,128)(2,1)S(1)} %pad_bitcast_fusion.id_ref), custom_call_target="tpu_custom_call" | custom-call | tf_op jit(solution)/shard_map/pack/pallas_call | solution.py:52
  4.5 0.0 slice-start
  4.5 0.0 slice-start.1
  4.5 58.9 %all_to_all.10.got = bf16[16,1072,128]{2,1,0:T(8,128)(2,1)S(1)} all-to-all(bf16[16,1072,128]{2,1,0:T(8,128)(2,1)S(1)} %pack.1), channel_id=1, replica_groups=mesh['dp'=8,'seq'=8,'mp'=2] {'seq','mp'}, dimensions={0} | all-to-all | bytes 8781824 | tf_op jit(solution)/shard_map/all_to_all | solution.py:312
  63.5 0.0 slice-start.2
  63.5 14.6 %attend.1 = bf16[16,576,128]{2,1,0:T(8,128)(2,1)S(1)} custom-call(s32[1]{0:T(128)} %bitcast.1.mp_ref, bf16[16,1072,128]{2,1,0:T(8,128)(2,1)S(1)} %all_to_all.10.got), custom_call_target="tpu_custom_call" | custom-call | tf_op jit(solution)/shard_map/attend/pallas_call | solution.py:182
  78.1 0.0 copy-start.1
  78.1 36.1 %all_to_all.11.got = bf16[16,576,128]{2,1,0:T(8,128)(2,1)S(1)} all-to-all(bf16[16,576,128]{2,1,0:T(8,128)(2,1)S(1)} %attend.1), channel_id=1, replica_groups=mesh['dp'=8,'seq'=8,'mp'=2] {'seq','mp'}, dimensions={0} | all-to-all | bytes 4718592 | tf_op jit(solution)/shard_map/all_to_all | solution.py:313
  114.2 0.0 slice-done
  114.2 0.0 slice-done.1
  114.2 0.0 slice-done.2
  114.2 0.0 copy-done.1
  114.2 5.9 %project.1 = (bf16[384,1536]{1,0:T(8,128)(2,1)}, f32[384,1536]{1,0:T(8,128)S(1)}, f32[8,384]{1,0:T(8,128)S(1)}) custom-call(bf16[16,576,128]{2,1,0:T(8,128)(2,1)S(1)} %all_to_all.11.got, bf16[3072,1536]{1,0:T(8,128)(2,1)S(1)} %bitcast.11, bf16[384,1536]{1,0:T(8,128)(2,1)S(1)} %copy-done.1, f32[3,1536]{1,0:T(4,128)S(1)} %bitcast.12), custom_call_target="tpu_custom_call" | custom-call | tf_op jit(solution)/shard_map/project/pallas_call | solution.py:253
  120.1 0.6 collective-permute-start
  120.7 4.7 %collective-permute-done.other_ref = f32[8,384]{1,0:T(8,128)S(1)} collective-permute-done((f32[8,384]{1,0:T(8,128)S(1)}, f32[8,384]{1,0:T(8,128)S(1)}, u32[]{:S(2)}, u32[]{:S(2)}) %collective-permute-start) | collective-permute-done | bytes 12320 | tf_op jit(solution)/shard_map/ppermute | solution.py:315
  125.4 1.6 %norm.1 = bf16[384,1536]{1,0:T(8,128)(2,1)} custom-call(f32[384,1536]{1,0:T(8,128)S(1)} %get-tuple-element.12.stream_ref, f32[8,384]{1,0:T(8,128)S(1)} %get-tuple-element.13.mine_ref, f32[8,384]{1,0:T(8,128)S(1)} %collective-permute-done.other_ref, f32[3,1536]{1,0:T(4,128)S(1)} %bitcast.13), custom_call_target="tpu_custom_call" | custom-call | tf_op jit(solution)/shard_map/norm/pallas_call | solution.py:292
  (4 shorter events, 0.0 us)
Async XLA Ops:
  0.6 1.4 %copy-start = (f32[50,3,1536]{2,0,1:T(8,128)S(1)}, f32[50,3,1536]{2,0,1:T(8,128)}, u32[]{:S(2)}) copy-start(f32[50,3,1536]{2,0,1:T(8,128)} %param.14) | copy-start | bytes 2764804
  4.5 109.7 %slice-start = ((s8[9437184]{0:T(1024)(128)(4,1)}), s8[4194304]{0:T(1024)(128)(4,1)S(1)}, s32[]{:S(2)}) async-start(s8[9437184]{0:T(1024)(128)(4,1)} %bitcast.10), calls=%async_computation.2 | async-start | bytes 8388608
  4.5 109.7 %slice-start.1 = ((s8[9437184]{0:T(1024)(128)(4,1)}), s8[4194304]{0:T(1024)(128)(4,1)S(1)}, s32[]{:S(2)}) async-start(s8[9437184]{0:T(1024)(128)(4,1)} %bitcast.10), calls=%async_computation.3 | async-start | bytes 8388608
  63.5 50.7 %slice-start.2 = ((s8[9437184]{0:T(1024)(128)(4,1)}), s8[1048576]{0:T(1024)(128)(4,1)S(1)}, s32[]{:S(2)}) async-start(s8[9437184]{0:T(1024)(128)(4,1)} %bitcast.10), calls=%async_computation.4 | async-start | bytes 2097152
  78.1 36.1 %copy-start.1 = (bf16[384,1536]{1,0:T(8,128)(2,1)S(1)}, bf16[384,1536]{1,0:T(8,128)(2,1)}, u32[]{:S(2)}) copy-start(bf16[384,1536]{1,0:T(8,128)(2,1)} %res_ref.1) | copy-start | bytes 3538948
  120.1 5.3 %collective-permute-start = (f32[8,384]{1,0:T(8,128)S(1)}, f32[8,384]{1,0:T(8,128)S(1)}, u32[]{:S(2)}, u32[]{:S(2)}) collective-permute-start(f32[8,384]{1,0:T(8,128)S(1)} %get-tuple-element.13.mine_ref), channel_id=1, source_target_pairs={{0,1},{1,0},{2,3},{3,2},{4,5},{5,4},{6,7},{7,6},{8,9},{9,8},{10,11... | collective-permute-start | bytes 36872 | tf_op jit(solution)/shard_map/ppermute | solution.py:315

commit v5 on v4

--- a/solution.py
+++ b/solution.py
@@ -14,8 +14,10 @@
 HALF = ROWS // 2
 TOKENS = SHARDS * ROWS
 QF, KF, KM, VF, VM, QM, ID = 0, 192, 384, 576, 768, 960, 1056
-SENT = 1072
+SENT = 1064
 BLOCK = 512
+PART = 384
+LATER = 8
 BACK = 3 * ROWS
 TILE = 512
 SPARE = -(-TILE // ROWS)
@@ -39,19 +41,20 @@
 
 def pack_kernel(q_ref, k_ref, v_ref, id_ref, out_ref, sem):
     given = (q_ref, k_ref, v_ref)
+    ids = id_ref[...].astype(F32).astype(BF16)
     for s in range(SHARDS // 2):
         for m in range(2):
             for which, to, count, row, head in pieces(s, m):
                 source = given[which].at[pl.ds(row, count), pl.ds(head * HEAD_DIM, HEAD_DIM)]
                 pltpu.make_async_copy(source, out_ref.at[2 * s + m, pl.ds(to, count)], sem).start()
-            pltpu.make_async_copy(id_ref, out_ref.at[2 * s + m, pl.ds(ID, SENT - ID)], sem).start()
-    pltpu.make_async_copy(out_ref, out_ref, sem).wait()
+            out_ref[2 * s + m, ID:] = ids
+    pltpu.make_async_copy(out_ref.at[:, pl.ds(0, ID)], out_ref.at[:, pl.ds(0, ID)], sem).wait()
 
 
 def pack(queries, keys, values, id_rows):
     return pl.pallas_call(
         pack_kernel,
-        in_specs=[pl.BlockSpec(memory_space=pltpu.HBM)] * 3 + [pl.BlockSpec(memory_space=pl.ANY)],
+        in_specs=[pl.BlockSpec(memory_space=pltpu.HBM)] * 3 + [pl.BlockSpec(memory_space=pltpu.VMEM)],
         out_specs=pl.BlockSpec(memory_space=pltpu.VMEM),
         out_shape=pltpu.VMEM((SHARDS, SENT, HEAD_DIM), BF16),
         scratch_shapes=[pltpu.SemaphoreType.DMA],
@@ -91,19 +94,20 @@
     high_of = jnp.where(lane == 0, c0, jnp.where(lane == 1, c1, jnp.where(lane == 2, c2, jnp.where(lane == 3, TOKENS, end))))
 
     def inside(first, count):
-        token = lax.broadcasted_iota(jnp.int32, (count, HEAD_DIM), 0) + first
-        return (token >= low_of) & (token < high_of)
+        row = lax.broadcasted_iota(jnp.int32, (count, HEAD_DIM), 0).astype(F32).astype(BF16)
+        low, high = (jnp.clip(x - first, -1, 255).astype(F32).astype(BF16) for x in (low_of, high_of))
+        return (row >= low) & (row < high)
 
     def fill(b, _):
         here = inside(b * ROWS, ROWS)
-        is_k[b] = jnp.where(here, 0.0, -BIG).astype(BF16)
-        is_q[b] = jnp.where(here, 1.0, 0.0).astype(BF16)
-        is_m[b] = jnp.where(inside(b * ROWS + mp_ref[0] * HALF, HALF), 1.0, 0.0).astype(BF16)
+        is_k[b] = jnp.where(here, BF16(0.0), BF16(-BIG))
+        is_q[b] = jnp.where(here, BF16(1.0), BF16(0.0))
+        is_m[b] = jnp.where(inside(b * ROWS + mp_ref[0] * HALF, HALF), BF16(1.0), BF16(0.0))
         return 0
 
-    lax.fori_loop(0, SHARDS, fill, 0)
+    lax.fori_loop(0, SHARDS, fill, 0, unroll=4)
     for b in range(SHARDS, SHARDS + SPARE):
-        is_k[b] = jnp.where(inside(b * ROWS, ROWS), 0.0, -BIG).astype(BF16)
+        is_k[b] = jnp.where(inside(b * ROWS, ROWS), BF16(0.0), BF16(-BIG))
     for copy in copies[1:]:
         copy.wait()
 
@@ -207,7 +211,14 @@
     )(mp_index, got)
 
 
-def project_kernel(got, w_ref, res_ref, mod_ref, hidden_hbm, stream_ref, stat_ref, attended, hidden, sums, sem):
+def pick(step, table):
+    row = lax.broadcasted_iota(jnp.int32, table.shape, 0)
+    return jnp.sum(jnp.where(row == step, table, 0.0), axis=0, keepdims=True)
+
+
+def project_kernel(small_ref, got, w_ref, res_ref, mod_ref, hidden_hbm, stream_ref, stat_ref, rows_ref, attended, hidden, gates, sums, sem):
+    blocks = w_ref.shape[1] // BLOCK
+    now = small_ref[SENT - ID - 1 :, HEAD_DIM - 1 :] - LATER
     for s in range(SHARDS // 2):
         mid = slice((3 * s + 1) * HEAD_DIM, (3 * s + 2) * HEAD_DIM)
         for m in range(2):
@@ -219,11 +230,14 @@
                     d, 2 * ROWS + b * HALF : 2 * ROWS + (b + 1) * HALF
                 ]
     sums[...] = jnp.zeros_like(sums)
+    gates[...] = pick(now, mod_ref[0])
+    rows_ref[0:1, :] = pick(now, mod_ref[1])
+    rows_ref[1:2, :] = 1.0 + pick(now, mod_ref[2])
 
     def body(j, _):
         block = pl.ds(pl.multiple_of(j * BLOCK, BLOCK), BLOCK)
         projected = jnp.dot(attended[...], w_ref[:, block], preferred_element_type=F32)
-        stream = res_ref[:, block].astype(F32) + mod_ref[0:1, block] * projected
+        stream = res_ref[:, block].astype(F32) + gates[:, block] * projected
         hidden[:, block] = stream.astype(BF16)
         stream_ref[:, block] = stream
         pltpu.make_async_copy(hidden.at[:, block], hidden_hbm.at[:, block], sem.at[j]).start()
@@ -236,7 +250,6 @@
         sums[1] = two
         return 0
 
-    blocks = w_ref.shape[1] // BLOCK
     lax.fori_loop(0, blocks, body, 0)
     stat_ref[...] = jnp.zeros_like(stat_ref)
     stat_ref[0:1, :] = jnp.sum(sums[0].T, axis=0, keepdims=True)
@@ -246,55 +259,67 @@
         pltpu.make_async_copy(hidden.at[:, at], hidden_hbm.at[:, at], sem.at[j]).wait()
 
 
-def project(got, out_weight, residual, mod_rows):
+def project(small, got, out_weight, residual, tables):
     width, cols = out_weight.shape
     rows = residual.shape[0]
     whole = pl.BlockSpec(memory_space=pltpu.VMEM)
     return pl.pallas_call(
         project_kernel,
-        in_specs=[whole] * 4,
-        out_specs=[pl.BlockSpec(memory_space=pl.ANY), whole, whole],
+        in_specs=[whole] * 5,
+        out_specs=[pl.BlockSpec(memory_space=pl.ANY), whole, whole, whole],
         out_shape=[
             jax.ShapeDtypeStruct((rows, cols), BF16),
             jax.ShapeDtypeStruct((rows, cols), F32),
             jax.ShapeDtypeStruct((8, rows), F32),
+            jax.ShapeDtypeStruct((8, cols), F32),
         ],
         scratch_shapes=[
             pltpu.VMEM((rows, width), BF16),
             pltpu.VMEM((rows, cols), BF16),
+            pltpu.VMEM((1, cols), F32),
             pltpu.VMEM((2, rows, HEAD_DIM), F32),
             pltpu.SemaphoreType.DMA((cols // BLOCK,)),
         ],
         compiler_params=pltpu.CompilerParams(vmem_limit_bytes=24 << 20),
         name="project",
-    )(got, out_weight, residual, mod_rows)
-
-
-def norm_kernel(width, stream_ref, mine_ref, other_ref, mod_ref, out_ref):
+    )(small, got, out_weight, residual, tables)
+
+
+def norm_kernel(width, stream_ref, mine_ref, other_ref, rows_ref, out_hbm, out, moments, sem):
     stats = mine_ref[...] + other_ref[...]
     mean = stats[0:1, :] / width
     var = stats[1:2, :] / width - mean * mean
     rows = mean.shape[1]
-    mean = jnp.broadcast_to(mean, (HEAD_DIM, rows)).T
-    inv = jnp.broadcast_to(lax.rsqrt(var + 1e-06), (HEAD_DIM, rows)).T
-    for c in range(stream_ref.shape[1] // HEAD_DIM):
-        at = slice(c * HEAD_DIM, (c + 1) * HEAD_DIM)
-        shift = mod_ref[1:2, at]
-        scale = mod_ref[2:3, at]
-        out_ref[:, at] = ((stream_ref[:, at] - mean) * inv * (1.0 + scale) + shift).astype(BF16)
+    moments[0] = jnp.broadcast_to(mean, (HEAD_DIM, rows)).T
+    moments[1] = jnp.broadcast_to(lax.rsqrt(var + 1e-06), (HEAD_DIM, rows)).T
+    parts = out.shape[1] // PART
+
+    def body(j, _):
+        for c in range(0, PART, HEAD_DIM):
+            at = pl.ds(pl.multiple_of(j * PART + c, HEAD_DIM), HEAD_DIM)
+            scaled = (stream_ref[:, at] - moments[0]) * moments[1] * rows_ref[1:2, at]
+            out[:, at] = (scaled + rows_ref[0:1, at]).astype(BF16)
+        part = pl.ds(pl.multiple_of(j * PART, PART), PART)
+        pltpu.make_async_copy(out.at[:, part], out_hbm.at[:, part], sem.at[j]).start()
+        return 0
+
+    lax.fori_loop(0, parts, body, 0)
+    for j in range(parts):
+        part = pl.ds(j * PART, PART)
+        pltpu.make_async_copy(out.at[:, part], out_hbm.at[:, part], sem.at[j]).wait()
 
 
 def norm(stream, mine, other, mod_rows, width):
-    rows, cols = stream.shape
-    block = 768
-    column = lambda j: (0, j)
-    whole = pl.BlockSpec((8, rows), lambda j: (0, 0))
     return pl.pallas_call(
         functools.partial(norm_kernel, width),
-        grid=(cols // block,),
-        in_specs=[pl.BlockSpec((rows, block), column), whole, whole, pl.BlockSpec((3, block), column)],
-        out_specs=pl.BlockSpec((rows, block), column),
-        out_shape=jax.ShapeDtypeStruct((rows, cols), BF16),
+        in_specs=[pl.BlockSpec(memory_space=pltpu.VMEM)] * 4,
+        out_specs=pl.BlockSpec(memory_space=pl.ANY),
+        out_shape=jax.ShapeDtypeStruct(stream.shape, BF16),
+        scratch_shapes=[
+            pltpu.VMEM(stream.shape, BF16),
+            pltpu.VMEM((2, stream.shape[0], HEAD_DIM), F32),
+            pltpu.SemaphoreType.DMA((stream.shape[1] // PART,)),
+        ],
         compiler_params=pltpu.CompilerParams(vmem_limit_bytes=12 << 20),
         name="norm",
     )(stream, mine, other, mod_rows)
@@ -302,16 +327,14 @@
 
 def local(residual, queries, keys, values, video_ids, timestep, modulation, out_weight):
     axes = ("seq", "mp")
-    mod_rows = lax.dynamic_index_in_dim(modulation, timestep[0], 0, keepdims=False)
-    spare = jnp.full(((SENT - ID) * HEAD_DIM - ROWS,), 7, jnp.int32)
-    id_rows = jnp.concatenate([video_ids, spare]).reshape(SENT - ID, HEAD_DIM).astype(BF16)
+    spare = jnp.full(((SENT - ID) * HEAD_DIM - ROWS - 1,), LATER, jnp.int32)
+    small = jnp.concatenate([video_ids, spare, timestep + LATER]).reshape(SENT - ID, HEAD_DIM)
     mp_index = lax.axis_index("mp").astype(jnp.int32).reshape(1)
-    packed, mp_index, mod_rows = lax.optimization_barrier(
-        (pack(queries, keys, values, id_rows), mp_index, mod_rows)
-    )
+    packed, mp_index = lax.optimization_barrier((pack(queries, keys, values, small), mp_index))
     got = lax.all_to_all(packed, axes, 0, 0)
     back = lax.all_to_all(attend(mp_index, got), axes, 0, 0)
-    hidden, stream, mine = project(back, out_weight, residual, mod_rows)
+    tables = modulation.transpose(1, 0, 2)
+    hidden, stream, mine, mod_rows = project(small, back, out_weight, residual, tables)
     other = lax.ppermute(mine, "mp", [(0, 1), (1, 0)])
     return hidden, norm(stream, mine, other, mod_rows, queries.shape[1])
 

time: 128 us -> 126 us (0.984); the launches traced: 127 us -> 127 us
  no operation moved by 1% of the time
where the time goes in v5:
time: 126 us; the launch traced here: 127 us
  blocking collectives  94.4 us (75%)
  Pallas kernels  25.5 us (20%)
  waiting for transfers between devices  5.19 us (4%)
  between operations  1.38 us (1%)
    all_to_all x1, blocking collectives, local(): got = lax.all_to_all(packed, axes, 0, 0)  58.7 us
    all_to_all x1, blocking collectives, local(): back = lax.all_to_all(attend(mp_index, got), axes, 0, 0)  35.8 us
    pallas_call x1, Pallas kernels, attend(): pl.pallas_call(attend_kernel, in_specs=[pl.BlockSpec(memory_space=pltpu.S...  15.7 us
    pallas_call x1, Pallas kernels, project(): pl.pallas_call(project_kernel, in_specs=[whole] * 5, out_specs=[pl.BlockS...  6.04 us
    ppermute x1, waiting for transfers between devices, local(): other = lax.ppermute(mine, 'mp', [(0, 1), (1, 0)])  5.19 us
  transfers between devices with their start and end apart: 1, of which 1 were waited for; matrix products, arithmetic and copies ran while one was open for 0% of the time, Pallas kernels for 0%

profile of v5, /device:TPU:38, one launch (start us, length us, event | category | flops | bytes accessed | tf_op | source)
XLA Modules:
  0.0 127.4 jit_solution(5245491197279447934)
XLA Ops:
  1.3 0.8 add_bitcast_fusion.id_ref.small_ref
  2.0 2.3 %pack.1 = bf16[16,1064,128]{2,1,0:T(8,128)(2,1)S(1)} custom-call(bf16[192,3072]{1,0:T(8,128)(2,1)} %q_ref.1, bf16[192,3072]{1,0:T(8,128)(2,1)} %k_ref.1, bf16[192,3072]{1,0:T(8,128)(2,1)} %v_ref.1, s32[8,128]{1,0:T(8,128)S(1)} %add_bitcast_fusion.id_ref.small_ref), custom_call_target="tpu_custom_call" | custom-call | tf_op jit(solution)/shard_map/pack/pallas_call | solution.py:55
  4.4 0.0 slice-start
  4.4 0.0 slice-start.1
  4.4 58.7 %all_to_all.10.got = bf16[16,1064,128]{2,1,0:T(8,128)(2,1)S(1)} all-to-all(bf16[16,1064,128]{2,1,0:T(8,128)(2,1)S(1)} %pack.1), channel_id=1, replica_groups=mesh['dp'=8,'seq'=8,'mp'=2] {'seq','mp'}, dimensions={0} | all-to-all | bytes 8716288 | tf_op jit(solution)/shard_map/all_to_all | solution.py:334
  63.1 0.0 slice-start.2
  63.1 15.7 %attend.1 = bf16[16,576,128]{2,1,0:T(8,128)(2,1)S(1)} custom-call(s32[1]{0:T(128)} %bitcast.1.mp_ref, bf16[16,1064,128]{2,1,0:T(8,128)(2,1)S(1)} %all_to_all.10.got), custom_call_target="tpu_custom_call" | custom-call | tf_op jit(solution)/shard_map/attend/pallas_call | solution.py:186
  78.8 0.0 copy-start
  78.8 0.0 copy-start.1
  78.8 35.8 %all_to_all.11.got = bf16[16,576,128]{2,1,0:T(8,128)(2,1)S(1)} all-to-all(bf16[16,576,128]{2,1,0:T(8,128)(2,1)S(1)} %attend.1), channel_id=1, replica_groups=mesh['dp'=8,'seq'=8,'mp'=2] {'seq','mp'}, dimensions={0} | all-to-all | bytes 4718592 | tf_op jit(solution)/shard_map/all_to_all | solution.py:335
  114.6 0.0 slice-done
  114.6 0.0 slice-done.1
  114.6 0.0 slice-done.2
  114.6 0.0 copy-done
  114.6 0.0 copy-done.1
  114.6 6.0 %project.1 = (bf16[384,1536]{1,0:T(8,128)(2,1)}, f32[384,1536]{1,0:T(8,128)S(1)}, f32[8,384]{1,0:T(8,128)S(1)}, f32[8,1536]{1,0:T(8,128)S(1)}) custom-call(s32[8,128]{1,0:T(8,128)S(1)} %add_bitcast_fusion.id_ref.small_ref, bf16[16,576,128]{2,1,0:T(8,128)(2,1)S(1)} %all_to_all.11.got, bf16[3072,1536]{1,0:T(8,128)(2,1)S(1)} %bitcast.5, ...), custom_call_target="tpu_custom_call" | custom-call | tf_op jit(solution)/shard_map/project/pallas_call | solution.py:266
  120.7 0.1 collective-permute-start
  120.8 5.2 %collective-permute-done.other_ref = f32[8,384]{1,0:T(8,128)S(1)} collective-permute-done((f32[8,384]{1,0:T(8,128)S(1)}, f32[8,384]{1,0:T(8,128)S(1)}, u32[]{:S(2)}, u32[]{:S(2)}) %collective-permute-start) | collective-permute-done | bytes 12320 | tf_op jit(solution)/shard_map/ppermute | solution.py:338
  125.9 1.5 %norm.1 = bf16[384,1536]{1,0:T(8,128)(2,1)} custom-call(f32[384,1536]{1,0:T(8,128)S(1)} %get-tuple-element.11.stream_ref, f32[8,384]{1,0:T(8,128)S(1)} %get-tuple-element.12.mine_ref, f32[8,384]{1,0:T(8,128)S(1)} %collective-permute-done.other_ref, f32[8,1536]{1,0:T(8,128)S(1)} %get-tuple-element.13.rows_ref), custom_call_target="tpu_custom_call" | custom-call | tf_op jit(solution)/shard_map/norm/pallas_call | solution.py:313
  (2 shorter events, 0.0 us)
Async XLA Ops:
  4.4 110.2 %slice-start = ((s8[9437184]{0:T(1024)(128)(4,1)}), s8[4194304]{0:T(1024)(128)(4,1)S(1)}, s32[]{:S(2)}) async-start(s8[9437184]{0:T(1024)(128)(4,1)} %bitcast.4), calls=%async_computation.2 | async-start | bytes 8388608
  4.4 110.2 %slice-start.1 = ((s8[9437184]{0:T(1024)(128)(4,1)}), s8[4194304]{0:T(1024)(128)(4,1)S(1)}, s32[]{:S(2)}) async-start(s8[9437184]{0:T(1024)(128)(4,1)} %bitcast.4), calls=%async_computation.3 | async-start | bytes 8388608
  63.1 51.5 %slice-start.2 = ((s8[9437184]{0:T(1024)(128)(4,1)}), s8[1048576]{0:T(1024)(128)(4,1)S(1)}, s32[]{:S(2)}) async-start(s8[9437184]{0:T(1024)(128)(4,1)} %bitcast.4), calls=%async_computation.4 | async-start | bytes 2097152
  78.8 35.8 %copy-start = (bf16[384,1536]{1,0:T(8,128)(2,1)S(1)}, bf16[384,1536]{1,0:T(8,128)(2,1)}, u32[]{:S(2)}) copy-start(bf16[384,1536]{1,0:T(8,128)(2,1)} %res_ref.1) | copy-start | bytes 3538948
  78.8 35.8 %copy-start.1 = (f32[50,3,1536]{2,0,1:T(8,128)S(1)}, f32[50,3,1536]{2,0,1:T(8,128)}, u32[]{:S(2)}) copy-start(f32[50,3,1536]{2,0,1:T(8,128)} %param.14) | copy-start | bytes 2764804
  120.7 5.3 %collective-permute-start = (f32[8,384]{1,0:T(8,128)S(1)}, f32[8,384]{1,0:T(8,128)S(1)}, u32[]{:S(2)}, u32[]{:S(2)}) collective-permute-start(f32[8,384]{1,0:T(8,128)S(1)} %get-tuple-element.12.mine_ref), channel_id=1, source_target_pairs={{0,1},{1,0},{2,3},{3,2},{4,5},{5,4},{6,7},{7,6},{8,9},{9,8},{10,11... | collective-permute-start | bytes 36872 | tf_op jit(solution)/shard_map/ppermute | solution.py:338
